TPU v7x, 256 devices: a whole 4x4x8 slice. The times are simulated.
256 devices in a mesh: gx: 4 (over x), gy: 4 (over z_lo, core), gz: 16 (over z_hi, y).
Axes of the slice: x: 4, y: 4, z: 8 (z_hi: 4, z_lo: 2; z = z_hi * 2 + z_lo), core: 2. Of those that a mesh axis runs over, the one named last changes fastest.
Arguments:
- flow_adjoint: float32 [19, 64, 64, 2048], P(None, 'gx', 'gy', 'gz'), may hold values from -6 to 6
- solute_adjoint: float32 [7, 64, 64, 2048], P(None, 'gx', 'gy', 'gz'), may hold values from -6 to 6
- flow_density: bfloat16 [4, 64, 64, 2048], P(None, 'gx', 'gy', 'gz'), may hold values from 0.796875 to 1.25
- flow_velocity: bfloat16 [4, 3, 64, 64, 2048], P(None, None, 'gx', 'gy', 'gz'), may hold values from -0.119628906 to 0.119628906
- solute_level: bfloat16 [4, 64, 64, 2048], P(None, 'gx', 'gy', 'gz'), may hold values from 0.099609375 to 3
- solid: int32 [64, 64, 2048], P('gx', 'gy', 'gz'), may hold values 0 or 1
- owner: int32 [64], replicated, may hold values from 0 to 15, as said below
Outputs:
- flow_result: float32 [19, 64, 64, 2048], P(None, 'gx', 'gy', 'gz')
- solute_result: float32 [7, 64, 64, 2048], P(None, 'gx', 'gy', 'gz')
Inputs may be any that keep to these rules, and one draw needn't show every extreme that they name: owner never falls along the list; every gz device holds 1 to 7 blocks.
All inputs are finite; a program needn't handle non-finite values. No bound on the sum of `solid` on one device may be relied on, other than what follows from the above.
Results may differ from a plain program's by a relative error of at most 0.0003.
Values sent between devices are 32-bit elements; how exact they have to be, the bound alone decides.
A program may use at most 128 MiB of HBM per device.

v0:
```python
import jax
import jax.numpy as jnp
from jax import lax
from jax.sharding import PartitionSpec as P

BZC = 16


FLOW_DIRS = [
    (0, 0, 0),
    (1, 0, 0),
    (-1, 0, 0),
    (0, 1, 0),
    (0, -1, 0),
    (0, 0, 1),
    (0, 0, -1),
    (1, 1, 0),
    (-1, -1, 0),
    (1, -1, 0),
    (-1, 1, 0),
    (1, 0, 1),
    (-1, 0, -1),
    (1, 0, -1),
    (-1, 0, 1),
    (0, 1, 1),
    (0, -1, -1),
    (0, 1, -1),
    (0, -1, 1),
]
FLOW_WEIGHTS = [1.0 / 3.0] + [1.0 / 18.0] * 6 + [1.0 / 36.0] * 12
SOLUTE_DIRS = FLOW_DIRS[:7]
SOLUTE_WEIGHTS = [0.25] + [0.125] * 6
flow_omega = 1.25
solute_omega = 1.6
langmuir_rate = 0.05


def shifted(shard, axis, by):
    length = lax.axis_size(axis)
    pairs = [(i, i + by) for i in range(length) if 0 <= i + by < length]
    return lax.ppermute(shard, axis, pairs)


def padded_2(shard, sides, width):
    for axis, dim in sides:
        size, length = (lax.axis_size(axis), shard.shape[dim])
        up = [(i, (i + 1) % size) for i in range(size - 1)]
        down = [(j, i) for i, j in up]
        last = lax.slice_in_dim(shard, length - width, length, axis=dim)
        initial = lax.slice_in_dim(shard, 0, width, axis=dim)
        before = lax.ppermute(last, axis, up)
        after = lax.ppermute(initial, axis, down)
        shard = jnp.concatenate([before, shard, after], axis=dim)
    return shard


def opposite(table):
    return [table.index((-entry[0], -entry[1], -entry[2])) for entry in table]


def extend(field, length):
    top_layer = lax.dynamic_slice_in_dim(field, length - 1, 1, 3)
    from_below = shifted(top_layer, "gz", 1)
    from_above = shifted(field[:, :, :, 0:1], "gz", -1)
    grown = jnp.concatenate([from_below, field, jnp.zeros_like(from_below)], axis=3)
    grown = lax.dynamic_update_slice_in_dim(grown, from_above, length + 1, 3)
    return padded_2(grown, (("gx", 1), ("gy", 2)), 1)


def reverse_stream(padded, solid_pad, table, reverse):
    width_x = padded.shape[1] - 2
    width_y = padded.shape[2] - 2
    width_z = padded.shape[3] - 2
    centre = padded[:, 1:-1, 1:-1, 1:-1]
    result_rows = []
    for number, (step_x, step_y, step_z) in enumerate(table):
        near = padded[
            number,
            1 + step_x : 1 + step_x + width_x,
            1 + step_y : 1 + step_y + width_y,
            1 + step_z : 1 + step_z + width_z,
        ]
        blocked = solid_pad[
            1 + step_x : 1 + step_x + width_x,
            1 + step_y : 1 + step_y + width_y,
            1 + step_z : 1 + step_z + width_z,
        ]
        result_rows.append(jnp.where(blocked == 0, near, centre[reverse[number]]))
    return jnp.stack(result_rows)


def solute_update(read, level, velocity):
    vel_x = velocity[0].astype(jnp.float32)
    vel_y = velocity[1].astype(jnp.float32)
    vel_z = velocity[2].astype(jnp.float32)
    level = level.astype(jnp.float32)
    moment_zero = 0.0
    moment_x = 0.0
    moment_y = 0.0
    moment_z = 0.0
    for number, (step_x, step_y, step_z) in enumerate(SOLUTE_DIRS):
        weighted = SOLUTE_WEIGHTS[number] * read[number]
        moment_zero = moment_zero + weighted
        moment_x = moment_x + step_x * weighted
        moment_y = moment_y + step_y * weighted
        moment_z = moment_z + step_z * weighted
    uptake = langmuir_rate / ((1.0 + level) * (1.0 + level))
    common = (
        solute_omega
        * (moment_zero + 4.0 * (moment_x * vel_x + moment_y * vel_y + moment_z * vel_z))
        - uptake * moment_zero
    )
    updated = jnp.stack(
        [(1.0 - solute_omega) * read[number] + common for number in range(len(SOLUTE_DIRS))]
    )
    factor = 4.0 * solute_omega * level
    pull = jnp.stack([factor * moment_x, factor * moment_y, factor * moment_z])
    return (updated, pull)


def flow_update(read, density, velocity, pull):
    vel_x = velocity[0].astype(jnp.float32)
    vel_y = velocity[1].astype(jnp.float32)
    vel_z = velocity[2].astype(jnp.float32)
    speed_sq = vel_x * vel_x + vel_y * vel_y + vel_z * vel_z
    moment_zero = 0.0
    moment_x = 0.0
    moment_y = 0.0
    moment_z = 0.0
    for number, (step_x, step_y, step_z) in enumerate(FLOW_DIRS):
        weighted = FLOW_WEIGHTS[number] * read[number]
        along = step_x * vel_x + step_y * vel_y + step_z * vel_z
        moment_zero = moment_zero + weighted * (1.0 - 4.5 * along * along + 1.5 * speed_sq)
        shared = 9.0 * weighted * along
        moment_x = moment_x + weighted * (3.0 * step_x - 3.0 * vel_x) + shared * step_x
        moment_y = moment_y + weighted * (3.0 * step_y - 3.0 * vel_y) + shared * step_y
        moment_z = moment_z + weighted * (3.0 * step_z - 3.0 * vel_z) + shared * step_z
    inverse_density = 1.0 / density.astype(jnp.float32)
    result_rows = []
    for number, (step_x, step_y, step_z) in enumerate(FLOW_DIRS):
        relax = moment_zero + step_x * moment_x + step_y * moment_y + step_z * moment_z
        source = (
            pull[0] * (step_x - vel_x) + pull[1] * (step_y - vel_y) + pull[2] * (step_z - vel_z)
        ) * inverse_density
        result_rows.append((1.0 - flow_omega) * read[number] + flow_omega * relax + source)
    return jnp.stack(result_rows)


def per_device(
    flow_adjoint, solute_adjoint, flow_density, flow_velocity, solute_level, solid, owner
):
    depth = solid.shape[2]
    column = lax.axis_index("gz")
    count = jnp.sum((owner == column).astype(jnp.int32))
    length = count * BZC
    live = jnp.arange(depth, dtype=jnp.int32) < length
    valid = jnp.where(live[None, None, :] & (solid == 0), 1.0, 0.0).astype(jnp.float32)
    live_mask = jnp.where(live, 1.0, 0.0).astype(jnp.float32)
    top_solid = lax.dynamic_slice_in_dim(solid, length - 1, 1, 2)
    solid_below = shifted(top_solid, "gz", 1)
    solid_above = shifted(solid[:, :, 0:1], "gz", -1)
    solid_grown = jnp.concatenate([solid_below, solid, jnp.zeros_like(solid_below)], axis=2)
    solid_grown = lax.dynamic_update_slice_in_dim(solid_grown, solid_above, length + 1, 2)
    solid_pad = padded_2(solid_grown, (("gx", 0), ("gy", 1)), 1)
    flow_reverse = opposite(FLOW_DIRS)
    solute_reverse = opposite(SOLUTE_DIRS)
    flow = flow_adjoint * live_mask
    solute = solute_adjoint * live_mask
    steps = flow_density.shape[0]
    pulls = [None] * steps
    for step in reversed(range(steps)):
        read = reverse_stream(extend(solute, length), solid_pad, SOLUTE_DIRS, solute_reverse)
        solute, pulls[step] = solute_update(read, solute_level[step], flow_velocity[step])
        solute = solute * valid
    for step in reversed(range(steps)):
        read = reverse_stream(extend(flow, length), solid_pad, FLOW_DIRS, flow_reverse)
        flow = flow_update(read, flow_density[step], flow_velocity[step], pulls[step]) * valid
    return (flow, solute)


def solution(mesh):
    in_specs = (
        P(None, "gx", "gy", "gz"),
        P(None, "gx", "gy", "gz"),
        P(None, "gx", "gy", "gz"),
        P(None, None, "gx", "gy", "gz"),
        P(None, "gx", "gy", "gz"),
        P("gx", "gy", "gz"),
        P(),
    )
    out_specs = (P(None, "gx", "gy", "gz"), P(None, "gx", "gy", "gz"))
    return jax.shard_map(
        per_device, mesh=mesh, in_specs=in_specs, out_specs=out_specs, check_vma=False
    )
```

profile of v0, /device:TPU:166, one launch (start us, length us, event | category | flops | bytes accessed | tf_op | source)
XLA Modules:
  0.0 603.2 jit_solution(18246167291653914690)
XLA Ops:
  7.8 6.6 %collective-permute-start.3 = (s32[16,16,1]{2,1,0:T(8,128)}, s32[16,16,1]{2,1,0:T(8,128)}, u32[]{:S(2)}, u32[]{:S(2)}) collective-permute-start(s32[16,16,1]{2,1,0:T(8,128)} %get-tuple-element.267), channel_id=1, source_target_pairs={{1,0},{2,1},{3,2},{4,3},{5,4},{6,5},{7,6},{8,7},{9,8},{10,9},{11,1... | collective-permute-start | bytes 3080 | tf_op jit(solution)/shard_map/ppermute | solution.py:41
  20.6 8.1 %collective-permute-start.13 = (f32[7,16,16,1]{2,1,3,0:T(8,128)}, f32[7,16,16,1]{2,1,3,0:T(8,128)}, u32[]{:S(2)}, u32[]{:S(2)}) collective-permute-start(f32[7,16,16,1]{2,1,3,0:T(8,128)} %copy.98), channel_id=1, source_target_pairs={{1,0},{2,1},{3,2},{4,3},{5,4},{6,5},{7,6},{8,7},{9,8},{10,9},{11,1... | collective-permute-start | bytes 21512 | tf_op jit(solution)/shard_map/ppermute | solution.py:41
  45.3 8.1 %collective-permute-start.1 = (f32[19,16,16,1]{0,2,3,1:T(8,128)}, f32[19,16,16,1]{0,2,3,1:T(8,128)}, u32[]{:S(2)}, u32[]{:S(2)}) collective-permute-start(f32[19,16,16,1]{0,2,3,1:T(8,128)} %copy.94), channel_id=1, source_target_pairs={{1,0},{2,1},{3,2},{4,3},{5,4},{6,5},{7,6},{8,7},{9,8},{10,9},{11,1... | collective-permute-start | bytes 58376 | tf_op jit(solution)/shard_map/ppermute | solution.py:41
  69.9 11.2 %dynamic_update_slice.29 = f32[7,16,16,130]{3,2,1,0:T(8,128)} dynamic-update-slice(f32[7,16,16,130]{3,2,1,0:T(8,128)} %maximum_maximum_fusion.4, f32[7,16,16,1]{3,2,1,0:T(8,128)S(1)} %copy.99, s32[]{:T(128)} %constant.154.clone.1, s32[]{:T(128)} %constant.154.clone.1, s32[]{:T(128)} %constant.154.clone.1, s32[]{:T(128)S(6)} %select_n.333) | dynamic-update-slice | bytes 14340 | tf_op jit(solution)/shard_map/dynamic_update_slice | solution.py:66
  81.1 4.7 copy.93
  85.8 5.4 maximum_maximum_fusion
  91.1 4.7 copy.95
  95.8 26.2 %dynamic_update_slice.27 = f32[19,16,16,130]{3,2,1,0:T(8,128)} dynamic-update-slice(f32[19,16,16,130]{3,2,1,0:T(8,128)} %maximum_maximum_fusion, f32[19,16,16,1]{3,2,1,0:T(8,128)} %copy.95, s32[]{:T(128)} %constant.154.clone.1, s32[]{:T(128)} %constant.154.clone.1, s32[]{:T(128)} %constant.154.clone.1, s32[]{:T(128)S(6)} %select_n.333) | dynamic-update-slice | bytes 38916 | tf_op jit(solution)/shard_map/dynamic_update_slice | solution.py:66
  158.3 5.8 constant_dynamic-update-slice_fusion.18
  173.1 8.1 %collective-permute-start.25 = (f32[7,16,16,1]{2,1,3,0:T(8,128)}, f32[7,16,16,1]{2,1,3,0:T(8,128)}, u32[]{:S(2)}, u32[]{:S(2)}) collective-permute-start(f32[7,16,16,1]{2,1,3,0:T(8,128)} %copy.106), channel_id=1, source_target_pairs={{1,0},{2,1},{3,2},{4,3},{5,4},{6,5},{7,6},{8,7},{9,8},{10,9},{11,1... | collective-permute-start | bytes 21512 | tf_op jit(solution)/shard_map/ppermute | solution.py:41
  196.3 8.4 %collective-permute-start.19 = (f32[19,16,16,1]{0,2,3,1:T(8,128)}, f32[19,16,16,1]{0,2,3,1:T(8,128)}, u32[]{:S(2)}, u32[]{:S(2)}) collective-permute-start(f32[19,16,16,1]{0,2,3,1:T(8,128)} %copy.102), channel_id=1, source_target_pairs={{1,0},{2,1},{3,2},{4,3},{5,4},{6,5},{7,6},{8,7},{9,8},{10,9},{11,1... | collective-permute-start | bytes 58376 | tf_op jit(solution)/shard_map/ppermute | solution.py:41
  212.8 10.7 %dynamic_update_slice.31 = f32[7,16,16,130]{3,2,1,0:T(8,128)} dynamic-update-slice(f32[7,16,16,130]{3,2,1,0:T(8,128)} %maximum_maximum_fusion.5, f32[7,16,16,1]{3,2,1,0:T(8,128)} %copy.107, s32[]{:T(128)} %constant.154.clone.1, s32[]{:T(128)} %constant.154.clone.1, s32[]{:T(128)} %constant.154.clone.1, s32[]{:T(128)S(6)} %select_n.333) | dynamic-update-slice | bytes 14340 | tf_op jit(solution)/shard_map/dynamic_update_slice | solution.py:66
  223.5 4.7 copy.101
  228.2 5.4 maximum_maximum_fusion.1
  233.6 4.7 copy.103
  238.2 26.2 %dynamic_update_slice.30 = f32[19,16,16,130]{3,2,1,0:T(8,128)} dynamic-update-slice(f32[19,16,16,130]{3,2,1,0:T(8,128)} %maximum_maximum_fusion.1, f32[19,16,16,1]{3,2,1,0:T(8,128)} %copy.103, s32[]{:T(128)} %constant.154.clone.1, s32[]{:T(128)} %constant.154.clone.1, s32[]{:T(128)} %constant.154.clone.1, s32[]{:T(128)S(6)} %select_n.333) | dynamic-update-slice | bytes 38916 | tf_op jit(solution)/shard_map/dynamic_update_slice | solution.py:66
  271.4 4.8 collective-permute-start.26
  297.4 5.3 constant_dynamic-update-slice_fusion.44
  313.4 8.3 %collective-permute-start.37 = (f32[7,16,16,1]{2,1,3,0:T(8,128)}, f32[7,16,16,1]{2,1,3,0:T(8,128)}, u32[]{:S(2)}, u32[]{:S(2)}) collective-permute-start(f32[7,16,16,1]{2,1,3,0:T(8,128)} %copy.114), channel_id=1, source_target_pairs={{1,0},{2,1},{3,2},{4,3},{5,4},{6,5},{7,6},{8,7},{9,8},{10,9},{11,1... | collective-permute-start | bytes 21512 | tf_op jit(solution)/shard_map/ppermute | solution.py:41
  343.3 8.3 %collective-permute-start.31 = (f32[19,16,16,1]{0,2,3,1:T(8,128)}, f32[19,16,16,1]{0,2,3,1:T(8,128)}, u32[]{:S(2)}, u32[]{:S(2)}) collective-permute-start(f32[19,16,16,1]{0,2,3,1:T(8,128)} %copy.110), channel_id=1, source_target_pairs={{1,0},{2,1},{3,2},{4,3},{5,4},{6,5},{7,6},{8,7},{9,8},{10,9},{11,1... | collective-permute-start | bytes 58376 | tf_op jit(solution)/shard_map/ppermute | solution.py:41
  359.8 10.7 %dynamic_update_slice.33 = f32[7,16,16,130]{3,2,1,0:T(8,128)} dynamic-update-slice(f32[7,16,16,130]{3,2,1,0:T(8,128)} %maximum_maximum_fusion.6, f32[7,16,16,1]{3,2,1,0:T(8,128)} %copy.115, s32[]{:T(128)} %constant.154.clone.1, s32[]{:T(128)} %constant.154.clone.1, s32[]{:T(128)} %constant.154.clone.1, s32[]{:T(128)S(6)} %select_n.333) | dynamic-update-slice | bytes 14340 | tf_op jit(solution)/shard_map/dynamic_update_slice | solution.py:66
  370.5 4.7 copy.109
  375.2 5.4 maximum_maximum_fusion.2
  385.2 26.1 %dynamic_update_slice.32 = f32[19,16,16,130]{3,2,1,0:T(8,128)} dynamic-update-slice(f32[19,16,16,130]{3,2,1,0:T(8,128)} %maximum_maximum_fusion.2, f32[19,16,16,1]{3,2,1,0:T(8,128)} %copy.111, s32[]{:T(128)} %constant.154.clone.1, s32[]{:T(128)} %constant.154.clone.1, s32[]{:T(128)} %constant.154.clone.1, s32[]{:T(128)S(6)} %select_n.333) | dynamic-update-slice | bytes 38916 | tf_op jit(solution)/shard_map/dynamic_update_slice | solution.py:66
  416.2 4.8 collective-permute-start.38
  442.2 5.3 constant_dynamic-update-slice_fusion.70
  458.2 8.3 %collective-permute-start.49 = (f32[7,16,16,1]{2,1,3,0:T(8,128)}, f32[7,16,16,1]{2,1,3,0:T(8,128)}, u32[]{:S(2)}, u32[]{:S(2)}) collective-permute-start(f32[7,16,16,1]{2,1,3,0:T(8,128)} %copy.122), channel_id=1, source_target_pairs={{1,0},{2,1},{3,2},{4,3},{5,4},{6,5},{7,6},{8,7},{9,8},{10,9},{11,1... | collective-permute-start | bytes 21512 | tf_op jit(solution)/shard_map/ppermute | solution.py:41
  488.1 8.1 %collective-permute-start.43 = (f32[19,16,16,1]{0,2,3,1:T(8,128)}, f32[19,16,16,1]{0,2,3,1:T(8,128)}, u32[]{:S(2)}, u32[]{:S(2)}) collective-permute-start(f32[19,16,16,1]{0,2,3,1:T(8,128)} %copy.118), channel_id=1, source_target_pairs={{1,0},{2,1},{3,2},{4,3},{5,4},{6,5},{7,6},{8,7},{9,8},{10,9},{11,1... | collective-permute-start | bytes 58376 | tf_op jit(solution)/shard_map/ppermute | solution.py:41
  504.5 10.7 %dynamic_update_slice.35 = f32[7,16,16,130]{3,2,1,0:T(8,128)} dynamic-update-slice(f32[7,16,16,130]{3,2,1,0:T(8,128)} %maximum_maximum_fusion.7, f32[7,16,16,1]{3,2,1,0:T(8,128)} %copy.123, s32[]{:T(128)} %constant.154.clone.1, s32[]{:T(128)} %constant.154.clone.1, s32[]{:T(128)} %constant.154.clone.1, s32[]{:T(128)S(6)} %select_n.333) | dynamic-update-slice | bytes 14340 | tf_op jit(solution)/shard_map/dynamic_update_slice | solution.py:66
  521.4 4.7 copy.117
  526.1 5.4 maximum_maximum_fusion.3
  536.1 26.2 %dynamic_update_slice.34 = f32[19,16,16,130]{3,2,1,0:T(8,128)} dynamic-update-slice(f32[19,16,16,130]{3,2,1,0:T(8,128)} %maximum_maximum_fusion.3, f32[19,16,16,1]{3,2,1,0:T(8,128)} %copy.119, s32[]{:T(128)} %constant.154.clone.1, s32[]{:T(128)} %constant.154.clone.1, s32[]{:T(128)} %constant.154.clone.1, s32[]{:T(128)S(6)} %select_n.333) | dynamic-update-slice | bytes 38916 | tf_op jit(solution)/shard_map/dynamic_update_slice | solution.py:66
  (471 shorter events, 303.3 us)
Async XLA Ops:
  4.3 40.9 %collective-permute-start.2 = (s32[16,16,1]{2,1,0:T(8,128)}, s32[16,16,1]{2,1,0:T(8,128)}, u32[]{:S(2)}, u32[]{:S(2)}) collective-permute-start(s32[16,16,1]{2,1,0:T(8,128)} %get-tuple-element.268), channel_id=1, source_target_pairs={{0,1},{1,2},{2,3},{3,4},{4,5},{5,6},{6,7},{7,8},{8,9},{9,10},{10,1... | collective-permute-start | bytes 3080 | tf_op jit(solution)/shard_map/ppermute | solution.py:41
  7.8 47.3 %collective-permute-start.3 = (s32[16,16,1]{2,1,0:T(8,128)}, s32[16,16,1]{2,1,0:T(8,128)}, u32[]{:S(2)}, u32[]{:S(2)}) collective-permute-start(s32[16,16,1]{2,1,0:T(8,128)} %get-tuple-element.267), channel_id=1, source_target_pairs={{1,0},{2,1},{3,2},{4,3},{5,4},{6,5},{7,6},{8,7},{9,8},{10,9},{11,1... | collective-permute-start | bytes 3080 | tf_op jit(solution)/shard_map/ppermute | solution.py:41
  17.3 44.1 %collective-permute-start.12 = (f32[7,16,16,1]{2,1,3,0:T(8,128)}, f32[7,16,16,1]{2,1,3,0:T(8,128)}, u32[]{:S(2)}, u32[]{:S(2)}) collective-permute-start(f32[7,16,16,1]{2,1,3,0:T(8,128)} %copy.96), channel_id=1, source_target_pairs={{0,1},{1,2},{2,3},{3,4},{4,5},{5,6},{6,7},{7,8},{8,9},{9,10},{10,1... | collective-permute-start | bytes 21512 | tf_op jit(solution)/shard_map/ppermute | solution.py:41
  20.6 47.7 %collective-permute-start.13 = (f32[7,16,16,1]{2,1,3,0:T(8,128)}, f32[7,16,16,1]{2,1,3,0:T(8,128)}, u32[]{:S(2)}, u32[]{:S(2)}) collective-permute-start(f32[7,16,16,1]{2,1,3,0:T(8,128)} %copy.98), channel_id=1, source_target_pairs={{1,0},{2,1},{3,2},{4,3},{5,4},{6,5},{7,6},{8,7},{9,8},{10,9},{11,1... | collective-permute-start | bytes 21512 | tf_op jit(solution)/shard_map/ppermute | solution.py:41
  37.9 43.2 %collective-permute-start = (f32[19,16,16,1]{0,2,3,1:T(8,128)}, f32[19,16,16,1]{0,2,3,1:T(8,128)}, u32[]{:S(2)}, u32[]{:S(2)}) collective-permute-start(f32[19,16,16,1]{0,2,3,1:T(8,128)} %copy.92), channel_id=1, source_target_pairs={{0,1},{1,2},{2,3},{3,4},{4,5},{5,6},{6,7},{7,8},{8,9},{9,10},{10,1... | collective-permute-start | bytes 58376 | tf_op jit(solution)/shard_map/ppermute | solution.py:41
  45.3 45.9 %collective-permute-start.1 = (f32[19,16,16,1]{0,2,3,1:T(8,128)}, f32[19,16,16,1]{0,2,3,1:T(8,128)}, u32[]{:S(2)}, u32[]{:S(2)}) collective-permute-start(f32[19,16,16,1]{0,2,3,1:T(8,128)} %copy.94), channel_id=1, source_target_pairs={{1,0},{2,1},{3,2},{4,3},{5,4},{6,5},{7,6},{8,7},{9,8},{10,9},{11,1... | collective-permute-start | bytes 58376 | tf_op jit(solution)/shard_map/ppermute | solution.py:41
  58.7 74.9 %collective-permute-start.4 = (s32[1,16,130]{2,1,0:T(8,128)S(1)}, s32[1,16,130]{2,1,0:T(8,128)S(1)}, u32[]{:S(2)}, u32[]{:S(2)}) collective-permute-start(s32[1,16,130]{2,1,0:T(8,128)S(1)} %get-tuple-element.266), channel_id=1, source_target_pairs={{64,0},{128,64},{192,128},{65,1},{129,65},{193,129},{66,2},{130,66... | collective-permute-start | bytes 24968 | tf_op jit(solution)/shard_map/ppermute | solution.py:52
  61.4 73.5 %collective-permute-start.6 = (s32[1,16,130]{2,1,0:T(8,128)S(1)}, s32[1,16,130]{2,1,0:T(8,128)S(1)}, u32[]{:S(2)}, u32[]{:S(2)}) collective-permute-start(s32[1,16,130]{2,1,0:T(8,128)S(1)} %get-tuple-element.265), channel_id=1, source_target_pairs={{0,64},{64,128},{128,192},{1,65},{65,129},{129,193},{2,66},{66,130... | collective-permute-start | bytes 24968 | tf_op jit(solution)/shard_map/ppermute | solution.py:51
  123.1 14.1 %collective-permute-start.5 = (f32[19,1,16,130]{3,2,1,0:T(8,128)S(1)}, f32[19,1,16,130]{3,2,1,0:T(8,128)S(1)}, u32[]{:S(2)}, u32[]{:S(2)}) collective-permute-start(f32[19,1,16,130]{3,2,1,0:T(8,128)S(1)} %get-tuple-element.225), channel_id=1, source_target_pairs={{64,0},{128,64},{192,128},{65,1},{129,65},{193,129},{66,2},{130,66... | collective-permute-start | bytes 474248 | tf_op jit(solution)/shard_map/ppermute | solution.py:52
  129.0 17.1 %collective-permute-start.14 = (f32[7,1,16,130]{3,2,1,0:T(8,128)S(1)}, f32[7,1,16,130]{3,2,1,0:T(8,128)S(1)}, u32[]{:S(2)}, u32[]{:S(2)}) collective-permute-start(f32[7,1,16,130]{3,2,1,0:T(8,128)S(1)} %get-tuple-element.249), channel_id=1, source_target_pairs={{64,0},{128,64},{192,128},{65,1},{129,65},{193,129},{66,2},{130,66... | collective-permute-start | bytes 174728 | tf_op jit(solution)/shard_map/ppermute | solution.py:52
  133.6 16.2 %collective-permute-start.15 = (f32[7,1,16,130]{3,2,1,0:T(8,128)S(1)}, f32[7,1,16,130]{3,2,1,0:T(8,128)S(1)}, u32[]{:S(2)}, u32[]{:S(2)}) collective-permute-start(f32[7,1,16,130]{3,2,1,0:T(8,128)S(1)} %get-tuple-element.248), channel_id=1, source_target_pairs={{0,64},{64,128},{128,192},{1,65},{65,129},{129,193},{2,66},{66,130... | collective-permute-start | bytes 174728 | tf_op jit(solution)/shard_map/ppermute | solution.py:51
  135.0 17.0 %collective-permute-start.10 = (s32[18,1,130]{2,1,0:T(1,128)S(1)}, s32[18,1,130]{2,1,0:T(1,128)S(1)}, u32[]{:S(2)}, u32[]{:S(2)}) collective-permute-start(s32[18,1,130]{2,1,0:T(1,128)S(1)} %get-tuple-element.263), channel_id=1, source_target_pairs={{0,16},{16,32},{32,48},{1,17},{17,33},{33,49},{2,18},{18,34},{34,5... | collective-permute-start | bytes 28088 | tf_op jit(solution)/shard_map/ppermute | solution.py:51
  137.2 17.4 %collective-permute-start.8 = (s32[18,1,130]{2,1,0:T(1,128)S(1)}, s32[18,1,130]{2,1,0:T(1,128)S(1)}, u32[]{:S(2)}, u32[]{:S(2)}) collective-permute-start(s32[18,1,130]{2,1,0:T(1,128)S(1)} %get-tuple-element.264), channel_id=1, source_target_pairs={{16,0},{32,16},{48,32},{17,1},{33,17},{49,33},{18,2},{34,18},{50,3... | collective-permute-start | bytes 28088 | tf_op jit(solution)/shard_map/ppermute | solution.py:52
  144.1 14.1 %collective-permute-start.11 = (f32[19,18,1,130]{3,2,1,0:T(1,128)S(1)}, f32[19,18,1,130]{3,2,1,0:T(1,128)S(1)}, u32[]{:S(2)}, u32[]{:S(2)}) collective-permute-start(f32[19,18,1,130]{3,2,1,0:T(1,128)S(1)} %get-tuple-element.216), channel_id=1, source_target_pairs={{0,16},{16,32},{32,48},{1,17},{17,33},{33,49},{2,18},{18,34},{34,5... | collective-permute-start | bytes 533528 | tf_op jit(solution)/shard_map/ppermute | solution.py:51
  169.8 34.9 %collective-permute-start.24 = (f32[7,16,16,1]{2,1,3,0:T(8,128)}, f32[7,16,16,1]{2,1,3,0:T(8,128)}, u32[]{:S(2)}, u32[]{:S(2)}) collective-permute-start(f32[7,16,16,1]{2,1,3,0:T(8,128)} %copy.104), channel_id=1, source_target_pairs={{0,1},{1,2},{2,3},{3,4},{4,5},{5,6},{6,7},{7,8},{8,9},{9,10},{10,1... | collective-permute-start | bytes 21512 | tf_op jit(solution)/shard_map/ppermute | solution.py:41
  173.1 37.3 %collective-permute-start.25 = (f32[7,16,16,1]{2,1,3,0:T(8,128)}, f32[7,16,16,1]{2,1,3,0:T(8,128)}, u32[]{:S(2)}, u32[]{:S(2)}) collective-permute-start(f32[7,16,16,1]{2,1,3,0:T(8,128)} %copy.106), channel_id=1, source_target_pairs={{1,0},{2,1},{3,2},{4,3},{5,4},{6,5},{7,6},{8,7},{9,8},{10,9},{11,1... | collective-permute-start | bytes 21512 | tf_op jit(solution)/shard_map/ppermute | solution.py:41
  190.3 33.2 %collective-permute-start.18 = (f32[19,16,16,1]{0,2,3,1:T(8,128)}, f32[19,16,16,1]{0,2,3,1:T(8,128)}, u32[]{:S(2)}, u32[]{:S(2)}) collective-permute-start(f32[19,16,16,1]{0,2,3,1:T(8,128)} %copy.100), channel_id=1, source_target_pairs={{0,1},{1,2},{2,3},{3,4},{4,5},{5,6},{6,7},{7,8},{8,9},{9,10},{10,1... | collective-permute-start | bytes 58376 | tf_op jit(solution)/shard_map/ppermute | solution.py:41
  196.3 37.3 %collective-permute-start.19 = (f32[19,16,16,1]{0,2,3,1:T(8,128)}, f32[19,16,16,1]{0,2,3,1:T(8,128)}, u32[]{:S(2)}, u32[]{:S(2)}) collective-permute-start(f32[19,16,16,1]{0,2,3,1:T(8,128)} %copy.102), channel_id=1, source_target_pairs={{1,0},{2,1},{3,2},{4,3},{5,4},{6,5},{7,6},{8,7},{9,8},{10,9},{11,1... | collective-permute-start | bytes 58376 | tf_op jit(solution)/shard_map/ppermute | solution.py:41
  271.4 16.1 %collective-permute-start.26 = (f32[7,1,16,130]{3,2,1,0:T(8,128)S(1)}, f32[7,1,16,130]{3,2,1,0:T(8,128)S(1)}, u32[]{:S(2)}, u32[]{:S(2)}) collective-permute-start(f32[7,1,16,130]{3,2,1,0:T(8,128)S(1)} %get-tuple-element.247), channel_id=1, source_target_pairs={{64,0},{128,64},{192,128},{65,1},{129,65},{193,129},{66,2},{130,66... | collective-permute-start | bytes 174728 | tf_op jit(solution)/shard_map/ppermute | solution.py:52
  283.1 14.0 %collective-permute-start.22 = (f32[19,18,1,130]{3,2,1,0:T(1,128)S(1)}, f32[19,18,1,130]{3,2,1,0:T(1,128)S(1)}, u32[]{:S(2)}, u32[]{:S(2)}) collective-permute-start(f32[19,18,1,130]{3,2,1,0:T(1,128)S(1)} %get-tuple-element.215), channel_id=1, source_target_pairs={{16,0},{32,16},{48,32},{17,1},{33,17},{49,33},{18,2},{34,18},{50,3... | collective-permute-start | bytes 533528 | tf_op jit(solution)/shard_map/ppermute | solution.py:52
  310.1 41.5 %collective-permute-start.36 = (f32[7,16,16,1]{2,1,3,0:T(8,128)}, f32[7,16,16,1]{2,1,3,0:T(8,128)}, u32[]{:S(2)}, u32[]{:S(2)}) collective-permute-start(f32[7,16,16,1]{2,1,3,0:T(8,128)} %copy.112), channel_id=1, source_target_pairs={{0,1},{1,2},{2,3},{3,4},{4,5},{5,6},{6,7},{7,8},{8,9},{9,10},{10,1... | collective-permute-start | bytes 21512 | tf_op jit(solution)/shard_map/ppermute | solution.py:41
  313.4 44.0 %collective-permute-start.37 = (f32[7,16,16,1]{2,1,3,0:T(8,128)}, f32[7,16,16,1]{2,1,3,0:T(8,128)}, u32[]{:S(2)}, u32[]{:S(2)}) collective-permute-start(f32[7,16,16,1]{2,1,3,0:T(8,128)} %copy.114), channel_id=1, source_target_pairs={{1,0},{2,1},{3,2},{4,3},{5,4},{6,5},{7,6},{8,7},{9,8},{10,9},{11,1... | collective-permute-start | bytes 21512 | tf_op jit(solution)/shard_map/ppermute | solution.py:41
  337.4 33.1 %collective-permute-start.30 = (f32[19,16,16,1]{0,2,3,1:T(8,128)}, f32[19,16,16,1]{0,2,3,1:T(8,128)}, u32[]{:S(2)}, u32[]{:S(2)}) collective-permute-start(f32[19,16,16,1]{0,2,3,1:T(8,128)} %copy.108), channel_id=1, source_target_pairs={{0,1},{1,2},{2,3},{3,4},{4,5},{5,6},{6,7},{7,8},{8,9},{9,10},{10,1... | collective-permute-start | bytes 58376 | tf_op jit(solution)/shard_map/ppermute | solution.py:41
  343.3 37.2 %collective-permute-start.31 = (f32[19,16,16,1]{0,2,3,1:T(8,128)}, f32[19,16,16,1]{0,2,3,1:T(8,128)}, u32[]{:S(2)}, u32[]{:S(2)}) collective-permute-start(f32[19,16,16,1]{0,2,3,1:T(8,128)} %copy.110), channel_id=1, source_target_pairs={{1,0},{2,1},{3,2},{4,3},{5,4},{6,5},{7,6},{8,7},{9,8},{10,9},{11,1... | collective-permute-start | bytes 58376 | tf_op jit(solution)/shard_map/ppermute | solution.py:41
  416.2 16.1 %collective-permute-start.38 = (f32[7,1,16,130]{3,2,1,0:T(8,128)S(1)}, f32[7,1,16,130]{3,2,1,0:T(8,128)S(1)}, u32[]{:S(2)}, u32[]{:S(2)}) collective-permute-start(f32[7,1,16,130]{3,2,1,0:T(8,128)S(1)} %get-tuple-element.245), channel_id=1, source_target_pairs={{64,0},{128,64},{192,128},{65,1},{129,65},{193,129},{66,2},{130,66... | collective-permute-start | bytes 174728 | tf_op jit(solution)/shard_map/ppermute | solution.py:52
  428.0 14.0 %collective-permute-start.34 = (f32[19,18,1,130]{3,2,1,0:T(1,128)S(1)}, f32[19,18,1,130]{3,2,1,0:T(1,128)S(1)}, u32[]{:S(2)}, u32[]{:S(2)}) collective-permute-start(f32[19,18,1,130]{3,2,1,0:T(1,128)S(1)} %get-tuple-element.213), channel_id=1, source_target_pairs={{16,0},{32,16},{48,32},{17,1},{33,17},{49,33},{18,2},{34,18},{50,3... | collective-permute-start | bytes 533528 | tf_op jit(solution)/shard_map/ppermute | solution.py:52
  454.9 41.3 %collective-permute-start.48 = (f32[7,16,16,1]{2,1,3,0:T(8,128)}, f32[7,16,16,1]{2,1,3,0:T(8,128)}, u32[]{:S(2)}, u32[]{:S(2)}) collective-permute-start(f32[7,16,16,1]{2,1,3,0:T(8,128)} %copy.120), channel_id=1, source_target_pairs={{0,1},{1,2},{2,3},{3,4},{4,5},{5,6},{6,7},{7,8},{8,9},{9,10},{10,1... | collective-permute-start | bytes 21512 | tf_op jit(solution)/shard_map/ppermute | solution.py:41
  458.2 43.8 %collective-permute-start.49 = (f32[7,16,16,1]{2,1,3,0:T(8,128)}, f32[7,16,16,1]{2,1,3,0:T(8,128)}, u32[]{:S(2)}, u32[]{:S(2)}) collective-permute-start(f32[7,16,16,1]{2,1,3,0:T(8,128)} %copy.122), channel_id=1, source_target_pairs={{1,0},{2,1},{3,2},{4,3},{5,4},{6,5},{7,6},{8,7},{9,8},{10,9},{11,1... | collective-permute-start | bytes 21512 | tf_op jit(solution)/shard_map/ppermute | solution.py:41
  482.2 39.2 %collective-permute-start.42 = (f32[19,16,16,1]{0,2,3,1:T(8,128)}, f32[19,16,16,1]{0,2,3,1:T(8,128)}, u32[]{:S(2)}, u32[]{:S(2)}) collective-permute-start(f32[19,16,16,1]{0,2,3,1:T(8,128)} %copy.116), channel_id=1, source_target_pairs={{0,1},{1,2},{2,3},{3,4},{4,5},{5,6},{6,7},{7,8},{8,9},{9,10},{10,1... | collective-permute-start | bytes 58376 | tf_op jit(solution)/shard_map/ppermute | solution.py:41
  488.1 43.3 %collective-permute-start.43 = (f32[19,16,16,1]{0,2,3,1:T(8,128)}, f32[19,16,16,1]{0,2,3,1:T(8,128)}, u32[]{:S(2)}, u32[]{:S(2)}) collective-permute-start(f32[19,16,16,1]{0,2,3,1:T(8,128)} %copy.118), channel_id=1, source_target_pairs={{1,0},{2,1},{3,2},{4,3},{5,4},{6,5},{7,6},{8,7},{9,8},{10,9},{11,1... | collective-permute-start | bytes 58376 | tf_op jit(solution)/shard_map/ppermute | solution.py:41
  516.8 45.5 %collective-permute-start.50 = (f32[7,1,16,130]{3,2,1,0:T(8,128)}, f32[7,1,16,130]{3,2,1,0:T(8,128)}, u32[]{:S(2)}, u32[]{:S(2)}) collective-permute-start(f32[7,1,16,130]{3,2,1,0:T(8,128)} %get-tuple-element.243), channel_id=1, source_target_pairs={{64,0},{128,64},{192,128},{65,1},{129,65},{193,129},{66,2},{130,66... | collective-permute-start | bytes 174728 | tf_op jit(solution)/shard_map/ppermute | solution.py:52
  519.9 42.5 %collective-permute-start.51 = (f32[7,1,16,130]{3,2,1,0:T(8,128)}, f32[7,1,16,130]{3,2,1,0:T(8,128)}, u32[]{:S(2)}, u32[]{:S(2)}) collective-permute-start(f32[7,1,16,130]{3,2,1,0:T(8,128)} %get-tuple-element.242), channel_id=1, source_target_pairs={{0,64},{64,128},{128,192},{1,65},{65,129},{129,193},{2,66},{66,130... | collective-permute-start | bytes 174728 | tf_op jit(solution)/shard_map/ppermute | solution.py:51
  (121 other events, 1898.5 us)
where the time goes:
time: 611 us; the launch traced here: 603 us
  local copies, waits for them, and re-layouts  280 us (46%)
  starting transfers between devices  184 us (30%)
  other arithmetic  107 us (18%)
  waiting for transfers between devices  27.7 us (5%)
    dynamic_update_slice x8, local copies, waits for them, and re-layouts, extend(): grown = lax.dynamic_update_slice_in_dim(grown, from_above, length + 1, 3)  148 us
    ppermute x18, starting transfers between devices, shifted(): return lax.ppermute(shard, axis, pairs)  91.1 us
    ppermute x18, starting transfers between devices, padded_2(): after = lax.ppermute(initial, axis, down)  59.4 us
    ppermute x16, local copies, waits for them, and re-layouts, shifted(): return lax.ppermute(shard, axis, pairs)  56.1 us
    unnamed x96, other arithmetic  42.8 us
    slice x16, local copies, waits for them, and re-layouts, extend(): from_above = shifted(field[:, :, :, 0:1], 'gz', -1)  37.6 us
    concatenate x8, other arithmetic, extend(): jnp.concatenate([from_below, field, jnp.zeros_like(from_below)], axis=3)  34.2 us
    ppermute x18, starting transfers between devices, padded_2(): before = lax.ppermute(last, axis, up)  33.6 us
  transfers between devices with their start and end apart: 54, of which 12 were waited for; matrix products, arithmetic and copies ran while one was open for 45% of the time, Pallas kernels for 0%

commit v1 on v0

v1 whole, which is shorter than its diff:
```python
import functools

import jax
import jax.numpy as jnp
from jax import lax
from jax.experimental import pallas as pl
from jax.experimental.pallas import tpu as pltpu
from jax.sharding import PartitionSpec as P

MESH = pl.DeviceIdType.MESH
BZC = 16

FLOW_DIRS = [
    (0, 0, 0),
    (1, 0, 0),
    (-1, 0, 0),
    (0, 1, 0),
    (0, -1, 0),
    (0, 0, 1),
    (0, 0, -1),
    (1, 1, 0),
    (-1, -1, 0),
    (1, -1, 0),
    (-1, 1, 0),
    (1, 0, 1),
    (-1, 0, -1),
    (1, 0, -1),
    (-1, 0, 1),
    (0, 1, 1),
    (0, -1, -1),
    (0, 1, -1),
    (0, -1, 1),
]
NF = 19
DIRS = FLOW_DIRS + FLOW_DIRS[:7]
NP = len(DIRS)
OPP = [FLOW_DIRS.index((-c[0], -c[1], -c[2])) for c in FLOW_DIRS]
OPP = OPP + [NF + o for o in OPP[:7]]
flow_omega = 1.25
solute_omega = 1.6
langmuir_rate = 0.05

FACE = [[[p for p in range(NP) if DIRS[p][a] == s] for s in (1, -1)] for a in range(3)]
NQ = 6
SPAN = 18
NBR = [c for c in FLOW_DIRS[1:] if c[2] and c[0]]
NBR += [c for c in FLOW_DIRS[1:] if c[2] and c[1]]
NBR += [c for c in FLOW_DIRS[1:] if c[2] and not c[0] and not c[1]]
NBR += [c for c in FLOW_DIRS[1:] if not c[2] and not (c[0] and c[1])]
NBR += [c for c in FLOW_DIRS[1:] if c[0] and c[1]]
XY = [c for c in NBR if c[0] and c[1]]
XZ = [c for c in NBR if c[0] and c[2]]
YZ = [c for c in NBR if c[1] and c[2]]
Y0 = 8


def side(step):
    return 0 if step > 0 else 1


def kernel(
    sizes,
    steps,
    owner_ref,
    flow_hbm,
    sol_hbm,
    rho_hbm,
    vel_hbm,
    lev_hbm,
    solid_hbm,
    oflow,
    osol,
    A,
    S,
    Zh,
    rho,
    vel,
    lev,
    solid,
    sx,
    sy,
    sz,
    sxy,
    syz,
    rx,
    ry,
    rz,
    rxy,
    rxz,
    ryz,
    in_sem,
    send_sem,
    recv_sem,
):
    WX, WY, D = solid.shape
    H = WY // 8
    names = ("gx", "gy", "gz")
    me = tuple(lax.axis_index(a) for a in names)

    copies = [
        pltpu.make_async_copy(
            flow_hbm, A.at[0, pl.ds(0, NF), pl.ds(1, WX), pl.ds(Y0, WY), :], in_sem.at[0]
        ),
        pltpu.make_async_copy(
            sol_hbm, A.at[0, pl.ds(NF, NP - NF), pl.ds(1, WX), pl.ds(Y0, WY), :], in_sem.at[1]
        ),
        pltpu.make_async_copy(solid_hbm, solid, in_sem.at[2]),
        pltpu.make_async_copy(rho_hbm, rho, in_sem.at[3]),
        pltpu.make_async_copy(vel_hbm, vel, in_sem.at[4]),
        pltpu.make_async_copy(lev_hbm, lev, in_sem.at[5]),
    ]
    for c in copies:
        c.start()

    def exists(c):
        ok = None
        for a in range(3):
            if c[a] > 0:
                t = me[a] < sizes[a] - 1
            elif c[a] < 0:
                t = me[a] > 0
            else:
                continue
            ok = t if ok is None else jnp.logical_and(ok, t)
        return ok

    def device(c):
        return tuple(me[a] + c[a] for a in range(3))

    def neg(c):
        return (-c[0], -c[1], -c[2])

    def clear(ref):
        ref[...] = jnp.zeros(ref.shape, ref.dtype)

    for s in range(steps):
        for ref in (rx, ry, rz, rxy, rxz, ryz):
            clear(ref.at[s])

    barrier = pltpu.get_barrier_semaphore()
    for c in NBR:

        @pl.when(exists(c))
        def _(c=c):
            pl.semaphore_signal(barrier, inc=1, device_id=device(c), device_id_type=MESH)

    n = [
        (me[a] > 0).astype(jnp.int32) + (me[a] < sizes[a] - 1).astype(jnp.int32) for a in range(3)
    ]
    pl.semaphore_wait(
        barrier, n[0] + n[1] + n[2] + n[0] * n[1] + n[0] * n[2] + n[1] * n[2]
    )

    count = jnp.int32(0)
    for i in range(owner_ref.shape[0]):
        count = count + (owner_ref[i] == me[2]).astype(jnp.int32)
    top = count * BZC - 1

    lane = lax.broadcasted_iota(jnp.int32, (8, D), 1)
    group = lane // SPAN
    within = lane - group * SPAN
    is_top = lane == top
    is_bottom = lane == 0

    def message(c, slot, first):
        nq = NQ + 1 if first else NQ
        i = NBR.index(c)
        if c in XY:
            d = XY.index(c)
            src, dst = sxy.at[slot, d, pl.ds(0, nq - NQ + 1)], rxy.at[slot, d, pl.ds(0, nq - NQ + 1)]
        elif c in XZ:
            src, dst = sz.at[slot, side(c[2])], rxz.at[slot, XZ.index(c)]
        elif c in YZ:
            d = YZ.index(c)
            src, dst = syz.at[slot, d], ryz.at[slot, d]
        elif c[0]:
            s = side(c[0])
            src, dst = sx.at[slot, s, pl.ds(0, nq)], rx.at[slot, s, pl.ds(0, nq)]
        elif c[1]:
            s = side(c[1])
            src, dst = sy.at[slot, s, pl.ds(0, nq)], ry.at[slot, s, pl.ds(0, nq)]
        else:
            s = side(c[2])
            src, dst = sz.at[slot, s], rz.at[slot, s]
        return pltpu.make_async_remote_copy(
            src_ref=src,
            dst_ref=dst,
            send_sem=send_sem.at[slot, i],
            recv_sem=recv_sem.at[slot, i],
            device_id=device(neg(c)),
            device_id_type=MESH,
        )

    def send(slot, first):
        for c in NBR:

            @pl.when(exists(neg(c)))
            def _(c=c):
                message(c, slot, first).start()

    def wait_recv(slot, first):
        for c in NBR:

            @pl.when(exists(c))
            def _(c=c):
                message(c, slot, first).wait_recv()

    def wait_send(slot, first):
        for c in NBR:

            @pl.when(exists(neg(c)))
            def _(c=c):
                message(c, slot, first).wait_send()

    def stage_rows(slot, x, q, s, value):
        row = value[0:1] if s == 0 else value[7:8]
        sy[slot, s, q, x] = row

    def pack(slot, x, s, h, values):
        acc = sz[slot, s, pl.ds(8 * h, 8), :]
        source = jnp.int32(0) if s == 0 else top
        put = acc
        for q, value in enumerate(values):
            moved = pltpu.roll(value, (q * SPAN + x + 1 - source + D) % D, 1)
            put = jnp.where((group == q) & (within == x + 1), moved, put)
        sz[slot, s, pl.ds(8 * h, 8), :] = put

    def stage_rest(slot, first, cur):
        for s in (0, 1):
            x = 1 if s == 0 else WX
            for q, p in enumerate(FACE[0][s]):
                sx[slot, s, q] = A[cur, p, x, pl.ds(Y0, WY), :]
            if first:
                sx[slot, s, NQ] = S[0, x, pl.ds(Y0, WY), :]
        for d, c in enumerate(XY):
            q = FACE[1][side(c[1])].index(FLOW_DIRS.index(c))
            x = 0 if c[0] > 0 else WX - 1
            sxy[slot, d, 0] = sy[slot, side(c[1]), q, x]
            if first:
                sxy[slot, d, 1] = sy[slot, side(c[1]), NQ, x]
        for d, c in enumerate(YZ):
            y = 0 if c[1] > 0 else WY - 1
            syz[slot, d] = sz[slot, side(c[2]), pl.ds(y, 1), :]

    def merge(slot, first, cur):
        for s in (0, 1):
            x = WX + 1 if s == 0 else 0
            for q, p in enumerate(FACE[0][s]):
                A[cur, p, x, pl.ds(Y0, WY), :] = rx[slot, s, q]
            if first:
                S[0, x, pl.ds(Y0, WY), :] = rx[slot, s, NQ]

        def rows(x, carry):
            for s in (0, 1):
                y = Y0 + WY if s == 0 else Y0 - 1
                for q, p in enumerate(FACE[1][s]):
                    A[cur, p, x + 1, pl.ds(y, 1), :] = ry[slot, s, q, x]
                if first:
                    S[0, x + 1, pl.ds(y, 1), :] = ry[slot, s, NQ, x]
            return carry

        lax.fori_loop(0, WX, rows, 0)
        for d, c in enumerate(XY):
            x = WX + 1 if c[0] > 0 else 0
            y = Y0 + WY if c[1] > 0 else Y0 - 1
            p = FLOW_DIRS.index(c)
            A[cur, p, x, pl.ds(y, 1), :] = rxy[slot, d, 0]
            if first:
                S[0, x, pl.ds(y, 1), :] = rxy[slot, d, 1]
        for s in (0, 1):
            zc = 1 if s == 0 else -1
            for h in range(H):
                part = pl.ds(8 * h, 8)
                v = rz[slot, s, part, :]
                up = pltpu.roll(rxz[slot, XZ.index((1, 0, zc)), part, :], SPAN - 2, 1)
                down = pltpu.roll(rxz[slot, XZ.index((-1, 0, zc)), part, :], D - (SPAN - 2), 1)
                v = jnp.where(within == SPAN - 1, up, v)
                v = jnp.where(within == 0, down, v)
                Zh[s, pl.ds(Y0 + 8 * h, 8), :] = v
            Zh[s, pl.ds(Y0 + WY, 1), :] = ryz[slot, YZ.index((0, 1, zc))]
            Zh[s, pl.ds(Y0 - 1, 1), :] = ryz[slot, YZ.index((0, -1, zc))]

    def halo_lane(s, q, x, start):
        target = top if s == 0 else jnp.int32(0)
        return pltpu.roll(
            Zh[s, pl.ds(start, 8), :], (target - (q * SPAN + x) + 2 * D) % D, 1
        )

    def along_z(value, s, q, x, start):
        moved = pltpu.roll(value, D - 1 if s == 0 else 1, 1)
        return jnp.where(is_top if s == 0 else is_bottom, halo_lane(s, q, x, start), moved)

    for c in copies[:3]:
        c.wait()

    clear(Zh)
    for part in (0, Y0 + WY):
        for x in range(WX + 2):
            S[0, x, pl.ds(part, 8), :] = jnp.zeros((8, D), jnp.float32)

    sz[...] = jnp.zeros(sz.shape, jnp.float32)

    def first_stage(x, carry):
        flags = solid[x].astype(jnp.float32)
        S[0, x + 1, pl.ds(Y0, WY), :] = flags
        for h in range(H):
            part = pl.ds(Y0 + 8 * h, 8)
            flag = flags[8 * h : 8 * h + 8]
            for s in (0, 1):
                if h == (0 if s == 0 else H - 1):
                    for q, p in enumerate(FACE[1][s]):
                        stage_rows(0, x, q, s, A[0, p, x + 1, part, :])
                    stage_rows(0, x, NQ, s, flag)
                pack(0, x, s, h, [A[0, p, x + 1, part, :] for p in FACE[2][s]] + [flag])
        return carry

    lax.fori_loop(0, WX, first_stage, 0)
    stage_rest(0, True, 0)
    send(0, True)
    for c in copies[3:]:
        c.wait()
    wait_recv(0, True)
    merge(0, True, 0)

    def flags_z(x, carry):
        for s in (0, 1):
            for start in (Y0 - 8, Y0, Y0 + 8, Y0 + WY):
                part = pl.ds(start, 8)
                S[1 + s, x, part, :] = along_z(S[0, x, part, :], s, NQ, x, start)
        return carry

    lax.fori_loop(0, WX + 2, flags_z, 0)

    def cell(k, cur, x, h, start, u, level, density):
        t = steps - 1 - k

        def read(p):
            c = DIRS[p]
            here = A[cur, p, x + 1 + c[0], pl.ds(start + c[1], 8), :]
            if c == (0, 0, 0):
                return here
            if c[2]:
                s = side(c[2])
                here = along_z(here, s, FACE[2][s].index(p), x + 1 + c[0], start + c[1])
                flag = S[1 + s, x + 1 + c[0], pl.ds(start + c[1], 8), :]
            else:
                flag = S[0, x + 1 + c[0], pl.ds(start + c[1], 8), :]
            back = A[cur, OPP[p], x + 1, pl.ds(start, 8), :]
            return jnp.where(flag > 0.5, back, here)

        ux, uy, uz = u
        new = [None] * NP
        h0 = read(NF)
        hs = [read(NF + p) for p in range(1, 7)]
        mx, my, mz = hs[0] - hs[1], hs[2] - hs[3], hs[4] - hs[5]
        m0 = 0.25 * h0 + 0.125 * ((hs[0] + hs[1]) + (hs[2] + hs[3]) + (hs[4] + hs[5]))
        along = mx * ux + my * uy + mz * uz
        one = 1.0 + level
        common = (solute_omega - langmuir_rate / (one * one)) * m0 + (
            solute_omega * 0.5
        ) * along
        for p, v in enumerate([h0] + hs):
            new[NF + p] = (1.0 - solute_omega) * v + common
        inverse = 1.0 / density
        factor = (0.5 * solute_omega) * level * inverse
        g = [read(p) for p in range(NF)]
        a = [g[p] + g[p + 1] for p in range(1, NF, 2)]
        d = [g[p] - g[p + 1] for p in range(1, NF, 2)]
        ax, ay, az = 2.0 * a[0], 2.0 * a[1], 2.0 * a[2]
        sxy_, sxz_, syz_ = a[3] + a[4], a[5] + a[6], a[7] + a[8]
        qxy, qxz, qyz = a[3] - a[4], a[5] - a[6], a[7] - a[8]
        qxx, qyy, qzz = ax + sxy_ + sxz_, ay + sxy_ + syz_, az + sxz_ + syz_
        total = 12.0 * g[0] + (qxx + ay + az) + syz_
        jx = 2.0 * d[0] + (d[3] + d[4]) + (d[5] + d[6])
        jy = 2.0 * d[1] + (d[3] - d[4]) + (d[7] + d[8])
        jz = 2.0 * d[2] + (d[5] - d[6]) + (d[7] - d[8])
        vx = qxx * ux + qxy * uy + qxz * uz
        vy = qxy * ux + qyy * uy + qyz * uz
        vz = qxz * ux + qyz * uy + qzz * uz
        quad = vx * ux + vy * uy + vz * uz
        speed = ux * ux + uy * uy + uz * uz
        w = flow_omega / 36.0
        scalar = w * (total * (1.0 + 1.5 * speed) - 4.5 * quad) - factor * along
        tx = (3.0 * w) * (jx + 3.0 * vx - ux * total) + factor * mx
        ty = (3.0 * w) * (jy + 3.0 * vy - uy * total) + factor * my
        tz = (3.0 * w) * (jz + 3.0 * vz - uz * total) + factor * mz
        rest = 1.0 - flow_omega
        new[0] = rest * g[0] + scalar
        pairs = [tx, ty, tz, tx + ty, tx - ty, tx + tz, tx - tz, ty + tz, ty - tz]
        for i, v in enumerate(pairs):
            p = 1 + 2 * i
            new[p] = rest * g[p] + (scalar + v)
            new[p + 1] = rest * g[p + 1] + (scalar - v)
        return new

    def slab(k, cur, x):
        t = steps - 1 - k
        level = lev[t, x].astype(jnp.float32)
        density = rho[t, x].astype(jnp.float32)
        u = [vel[t, i, x].astype(jnp.float32) for i in range(3)]
        for h in range(H):
            cut = slice(8 * h, 8 * h + 8)
            yield h, cell(
                k, cur, x, h, Y0 + 8 * h, [v[cut] for v in u], level[cut], density[cut]
            )

    def step(k, carry):
        cur = lax.rem(k, 2)
        nxt = 1 - cur

        def body(x, carry):
            for h, new in slab(k, cur, x):
                part = pl.ds(Y0 + 8 * h, 8)
                for p in range(NP):
                    A[nxt, p, x + 1, part, :] = new[p]
                for s in (0, 1):
                    if h == (0 if s == 0 else H - 1):
                        for q, p in enumerate(FACE[1][s]):
                            stage_rows(k + 1, x, q, s, new[p])
                    pack(k + 1, x, s, h, [new[p] for p in FACE[2][s]])
            return carry

        lax.fori_loop(0, WX, body, 0)
        stage_rest(k + 1, False, nxt)
        send(k + 1, False)
        wait_recv(k + 1, False)
        merge(k + 1, False, nxt)
        return carry

    lax.fori_loop(0, steps - 1, step, 0)

    def last(x, carry):
        k = steps - 1
        for h, new in slab(k, k % 2, x):
            part = pl.ds(8 * h, 8)
            keep = (S[0, x + 1, pl.ds(Y0 + 8 * h, 8), :] < 0.5) & (lane <= top)
            for p in range(NP):
                value = jnp.where(keep, new[p], 0.0)
                if p < NF:
                    oflow[p, x, part, :] = value
                else:
                    osol[p - NF, x, part, :] = value
        return carry

    lax.fori_loop(0, WX, last, 0)
    for s in range(steps):
        wait_send(s, s == 0)


def solution(mesh):
    names = ("gx", "gy", "gz")
    sizes = tuple(mesh.shape[a] for a in names)

    def per_device(flow, solute, rho, vel, lev, solid, owner):
        WX, WY, D = solid.shape
        steps = rho.shape[0]
        f32 = jnp.float32
        V = pltpu.VMEM
        DMA = pltpu.SemaphoreType.DMA
        hbm = pl.BlockSpec(memory_space=pl.ANY)
        n = len(NBR)
        return pl.pallas_call(
            functools.partial(kernel, sizes, steps),
            out_shape=(
                jax.ShapeDtypeStruct(flow.shape, f32),
                jax.ShapeDtypeStruct(solute.shape, f32),
            ),
            in_specs=[pl.BlockSpec(memory_space=pltpu.SMEM)] + [hbm] * 6,
            out_specs=(pl.BlockSpec(memory_space=pltpu.VMEM),) * 2,
            scratch_shapes=[
                V((2, NP, WX + 2, WY + 16, D), f32),
                V((3, WX + 2, WY + 16, D), f32),
                V((2, WY + 16, D), f32),
                V(rho.shape, rho.dtype),
                V(vel.shape, vel.dtype),
                V(lev.shape, lev.dtype),
                V(solid.shape, solid.dtype),
                V((steps, 2, NQ + 1, WY, D), f32),
                V((steps, 2, NQ + 1, WX, 1, D), f32),
                V((steps, 2, WY, D), f32),
                V((steps, 4, 2, 1, D), f32),
                V((steps, 4, 1, D), f32),
                V((steps, 2, NQ + 1, WY, D), f32),
                V((steps, 2, NQ + 1, WX, 1, D), f32),
                V((steps, 2, WY, D), f32),
                V((steps, 4, 2, 1, D), f32),
                V((steps, 4, WY, D), f32),
                V((steps, 4, 1, D), f32),
                DMA((6,)),
                DMA((steps, n)),
                DMA((steps, n)),
            ],
            compiler_params=pltpu.CompilerParams(
                collective_id=0, has_side_effects=True, vmem_limit_bytes=60 * 2**20
            ),
        )(owner, flow, solute, rho, vel, lev, solid)

    field = P(None, "gx", "gy", "gz")
    return jax.shard_map(
        per_device,
        mesh=mesh,
        in_specs=(field, field, field, P(None, None, "gx", "gy", "gz"), field, P("gx", "gy", "gz"), P()),
        out_specs=(field, field),
        check_vma=False,
    )
```

time: 611 us -> 59.4 us (0.10)
  the two profiles are of different devices: /device:TPU:166 before, /device:TPU:88 now
where the time goes in v1:
time: 59.4 us; the launch traced here: 59.3 us
  Pallas kernels  54.3 us (91%)
  local copies, waits for them, and re-layouts  4.38 us (7%)
  between operations  0.65 us (1%)
    pallas_call x1, Pallas kernels, per_device(): pl.pallas_call(functools.partial(kernel, sizes, steps), out_shape=(jax.Sh...  54.3 us
    unnamed x4, local copies, waits for them, and re-layouts  4.38 us

profile of v1, /device:TPU:88, one launch (start us, length us, event | category | flops | bytes accessed | tf_op | source)
XLA Modules:
  0.0 59.3 jit_solution(5430270664318590637)
XLA Ops:
  0.6 54.3 %shard_map.86 = (f32[19,16,16,128]{3,2,1,0:T(8,128)}, f32[7,16,16,128]{3,2,1,0:T(8,128)}) custom-call(s32[64]{0:T(128)} %owner_ref.1, f32[19,16,16,128]{3,2,1,0:T(8,128)} %flow_hbm.1, f32[7,16,16,128]{3,2,1,0:T(8,128)} %sol_hbm.1, bf16[4,16,16,128]{3,2,1,0:T(8,128)(2,1)} %rho_hbm.1, bf16[4,3,16,16,128]{4,3,2,1,0:T(8,128)(2,1)} %vel_hbm.1, ...), custom_call_target="tpu_custom_call" | custom-call | tf_op jit(solution)/shard_map/pallas_call | solution.py:462
  54.9 0.0 copy-start
  54.9 3.4 %copy.11 = f32[19,16,16,128]{3,2,1,0:T(8,128)} copy(f32[19,16,16,128]{3,2,1,0:T(8,128)} %get-tuple-element.4) | data formatting | bytes 4980736
  58.4 0.0 copy-done
  58.4 0.9 %copy.12 = f32[7,16,16,128]{3,2,1,0:T(8,128)} copy(f32[7,16,16,128]{3,2,1,0:T(8,128)S(1)} %copy-done) | data formatting | bytes 1835008
Async XLA Ops:
  54.9 3.5 %copy-start = (f32[7,16,16,128]{3,2,1,0:T(8,128)S(1)}, f32[7,16,16,128]{3,2,1,0:T(8,128)}, u32[]{:S(2)}) copy-start(f32[7,16,16,128]{3,2,1,0:T(8,128)} %get-tuple-element.5) | copy-start | bytes 2752516

commit v2 on v1

--- a/solution.py
+++ b/solution.py
@@ -42,7 +42,7 @@
 
 FACE = [[[p for p in range(NP) if DIRS[p][a] == s] for s in (1, -1)] for a in range(3)]
 NQ = 6
-SPAN = 18
+SPAN = 16
 NBR = [c for c in FLOW_DIRS[1:] if c[2] and c[0]]
 NBR += [c for c in FLOW_DIRS[1:] if c[2] and c[1]]
 NBR += [c for c in FLOW_DIRS[1:] if c[2] and not c[0] and not c[1]]
@@ -72,7 +72,6 @@
     osol,
     A,
     S,
-    Zh,
     rho,
     vel,
     lev,
@@ -130,13 +129,6 @@
     def neg(c):
         return (-c[0], -c[1], -c[2])
 
-    def clear(ref):
-        ref[...] = jnp.zeros(ref.shape, ref.dtype)
-
-    for s in range(steps):
-        for ref in (rx, ry, rz, rxy, rxz, ryz):
-            clear(ref.at[s])
-
     barrier = pltpu.get_barrier_semaphore()
     for c in NBR:
 
@@ -157,10 +149,28 @@
     top = count * BZC - 1
 
     lane = lax.broadcasted_iota(jnp.int32, (8, D), 1)
-    group = lane // SPAN
-    within = lane - group * SPAN
-    is_top = lane == top
-    is_bottom = lane == 0
+    row = lax.broadcasted_iota(jnp.int32, (8, D), 0)
+    halo_lane = (lane == top + 1, lane == D - 1)
+    slot_lane = (lane - (SPAN - 1), (lane - (top + SPAN - 1) + 2 * D) % D)
+
+    def landing(c, slot):
+        if c in XY:
+            return rxy.at[slot, XY.index(c)]
+        if c in XZ:
+            return rxz.at[slot, XZ.index(c)]
+        if c in YZ:
+            return ryz.at[slot, YZ.index(c)]
+        a = [i for i in range(3) if c[i]][0]
+        return (rx, ry, rz)[a].at[slot, side(c[a])]
+
+    def clear_missing():
+        for c in NBR:
+
+            @pl.when(jnp.logical_not(exists(c)))
+            def _(c=c):
+                for k in range(steps):
+                    ref = landing(c, k)
+                    ref[...] = jnp.zeros(ref.shape, ref.dtype)
 
     def message(c, slot, first):
         nq = NQ + 1 if first else NQ
@@ -212,20 +222,25 @@
             def _(c=c):
                 message(c, slot, first).wait_send()
 
-    def stage_rows(slot, x, q, s, value):
-        row = value[0:1] if s == 0 else value[7:8]
-        sy[slot, s, q, x] = row
-
-    def pack(slot, x, s, h, values):
-        acc = sz[slot, s, pl.ds(8 * h, 8), :]
-        source = jnp.int32(0) if s == 0 else top
-        put = acc
+    def stage_row(slot, x, q, s, value):
+        sy[slot, s, q, pl.ds(x, 1), :] = value[0:1] if s == 0 else value[7:8]
+
+    def pack(acc, s, values):
+        acc = pltpu.roll(acc, D - 1, 1)
         for q, value in enumerate(values):
-            moved = pltpu.roll(value, (q * SPAN + x + 1 - source + D) % D, 1)
-            put = jnp.where((group == q) & (within == x + 1), moved, put)
-        sz[slot, s, pl.ds(8 * h, 8), :] = put
-
-    def stage_rest(slot, first, cur):
+            moved = pltpu.roll(value, q * SPAN + SPAN - 1, 1)
+            acc = jnp.where(slot_lane[s] == q * SPAN, moved, acc)
+        return acc
+
+    def stage_rest(slot, first, cur, packed):
+        for i, (s, h) in enumerate((s, h) for s in (0, 1) for h in range(H)):
+            face = packed[i]
+            if s == 1:
+                face = pltpu.roll(face, D - top, 1)
+            sz[slot, s, pl.ds(8 * h, 8), :] = face
+            for d, c in enumerate(YZ):
+                if side(c[2]) == s and h == (0 if c[1] > 0 else H - 1):
+                    syz[slot, d] = face[0:1] if c[1] > 0 else face[7:8]
         for s in (0, 1):
             x = 1 if s == 0 else WX
             for q, p in enumerate(FACE[0][s]):
@@ -235,72 +250,79 @@
         for d, c in enumerate(XY):
             q = FACE[1][side(c[1])].index(FLOW_DIRS.index(c))
             x = 0 if c[0] > 0 else WX - 1
-            sxy[slot, d, 0] = sy[slot, side(c[1]), q, x]
+            sxy[slot, d, 0] = sy[slot, side(c[1]), q, pl.ds(x, 1), :]
             if first:
-                sxy[slot, d, 1] = sy[slot, side(c[1]), NQ, x]
-        for d, c in enumerate(YZ):
-            y = 0 if c[1] > 0 else WY - 1
-            syz[slot, d] = sz[slot, side(c[2]), pl.ds(y, 1), :]
+                sxy[slot, d, 1] = sy[slot, side(c[1]), NQ, pl.ds(x, 1), :]
 
     def merge(slot, first, cur):
+        flag = [(NQ, None)] if first else []
+
+        def put(p, x, rows, value):
+            if p is None:
+                S[0, x, rows, :] = value
+            else:
+                A[cur, p, x, rows, :] = value
+
         for s in (0, 1):
             x = WX + 1 if s == 0 else 0
-            for q, p in enumerate(FACE[0][s]):
-                A[cur, p, x, pl.ds(Y0, WY), :] = rx[slot, s, q]
-            if first:
-                S[0, x, pl.ds(Y0, WY), :] = rx[slot, s, NQ]
-
-        def rows(x, carry):
-            for s in (0, 1):
-                y = Y0 + WY if s == 0 else Y0 - 1
-                for q, p in enumerate(FACE[1][s]):
-                    A[cur, p, x + 1, pl.ds(y, 1), :] = ry[slot, s, q, x]
-                if first:
-                    S[0, x + 1, pl.ds(y, 1), :] = ry[slot, s, NQ, x]
-            return carry
-
-        lax.fori_loop(0, WX, rows, 0)
+            cx = 1 if s == 0 else -1
+            edge = 0 if s == 0 else WX - 1
+            for q, p in list(enumerate(FACE[0][s])) + flag:
+                for h in range(H):
+                    value = rx[slot, s, q, pl.ds(8 * h, 8), :]
+                    for z in (0, 1):
+                        cz = 1 - 2 * z
+                        if p is None or DIRS[p] == (cx, 0, cz) and p < NF:
+                            qz = NQ if p is None else FACE[2][z].index(p)
+                            line = rxz[slot, XZ.index((cx, 0, cz)), pl.ds(8 * h, 8), :]
+                            column = qz * SPAN + edge
+                            line = jnp.broadcast_to(line[:, column : column + 1], (8, D))
+                            value = jnp.where(halo_lane[z], line, value)
+                    put(p, x, pl.ds(Y0 + 8 * h, 8), value)
+        for s in (0, 1):
+            y = Y0 + WY if s == 0 else Y0 - 1
+            cy = 1 if s == 0 else -1
+            for q, p in list(enumerate(FACE[1][s])) + flag:
+                for half in range(WX // 8):
+                    value = ry[slot, s, q, pl.ds(8 * half, 8), :]
+                    for z in (0, 1):
+                        cz = 1 - 2 * z
+                        if p is None or DIRS[p] == (0, cy, cz) and p < NF:
+                            qz = NQ if p is None else FACE[2][z].index(p)
+                            line = jnp.broadcast_to(ryz[slot, YZ.index((0, cy, cz))], (8, D))
+                            here = lane == row + (qz * SPAN + 8 * half)
+                            line = jnp.sum(jnp.where(here, line, 0.0), axis=1, keepdims=True)
+                            value = jnp.where(halo_lane[z], line, value)
+                    for i in range(8):
+                        put(p, 1 + 8 * half + i, pl.ds(y, 1), value[i : i + 1])
         for d, c in enumerate(XY):
             x = WX + 1 if c[0] > 0 else 0
             y = Y0 + WY if c[1] > 0 else Y0 - 1
-            p = FLOW_DIRS.index(c)
-            A[cur, p, x, pl.ds(y, 1), :] = rxy[slot, d, 0]
+            put(FLOW_DIRS.index(c), x, pl.ds(y, 1), rxy[slot, d, 0])
             if first:
-                S[0, x, pl.ds(y, 1), :] = rxy[slot, d, 1]
+                put(None, x, pl.ds(y, 1), rxy[slot, d, 1])
         for s in (0, 1):
-            zc = 1 if s == 0 else -1
             for h in range(H):
-                part = pl.ds(8 * h, 8)
-                v = rz[slot, s, part, :]
-                up = pltpu.roll(rxz[slot, XZ.index((1, 0, zc)), part, :], SPAN - 2, 1)
-                down = pltpu.roll(rxz[slot, XZ.index((-1, 0, zc)), part, :], D - (SPAN - 2), 1)
-                v = jnp.where(within == SPAN - 1, up, v)
-                v = jnp.where(within == 0, down, v)
-                Zh[s, pl.ds(Y0 + 8 * h, 8), :] = v
-            Zh[s, pl.ds(Y0 + WY, 1), :] = ryz[slot, YZ.index((0, 1, zc))]
-            Zh[s, pl.ds(Y0 - 1, 1), :] = ryz[slot, YZ.index((0, -1, zc))]
-
-    def halo_lane(s, q, x, start):
-        target = top if s == 0 else jnp.int32(0)
-        return pltpu.roll(
-            Zh[s, pl.ds(start, 8), :], (target - (q * SPAN + x) + 2 * D) % D, 1
-        )
-
-    def along_z(value, s, q, x, start):
-        moved = pltpu.roll(value, D - 1 if s == 0 else 1, 1)
-        return jnp.where(is_top if s == 0 else is_bottom, halo_lane(s, q, x, start), moved)
+                rows = pl.ds(Y0 + 8 * h, 8)
+                face = rz[slot, s, pl.ds(8 * h, 8), :]
+                face = pltpu.roll(face, top + 1 if s == 0 else D - 1, 1)
+                for q, p in list(enumerate(FACE[2][s])) + flag:
+                    for x in range(WX):
+                        moved = pltpu.roll(face, D - (q * SPAN + x), 1) if q + x else face
+                        old = S[0, x + 1, rows, :] if p is None else A[cur, p, x + 1, rows, :]
+                        put(p, x + 1, rows, jnp.where(halo_lane[s], moved, old))
 
     for c in copies[:3]:
         c.wait()
 
-    clear(Zh)
     for part in (0, Y0 + WY):
         for x in range(WX + 2):
             S[0, x, pl.ds(part, 8), :] = jnp.zeros((8, D), jnp.float32)
 
-    sz[...] = jnp.zeros(sz.shape, jnp.float32)
-
-    def first_stage(x, carry):
+    blank = (jnp.zeros((8, D), jnp.float32),) * (2 * H)
+
+    def first_stage(x, packed):
+        packed = list(packed)
         flags = solid[x].astype(jnp.float32)
         S[0, x + 1, pl.ds(Y0, WY), :] = flags
         for h in range(H):
@@ -309,24 +331,28 @@
             for s in (0, 1):
                 if h == (0 if s == 0 else H - 1):
                     for q, p in enumerate(FACE[1][s]):
-                        stage_rows(0, x, q, s, A[0, p, x + 1, part, :])
-                    stage_rows(0, x, NQ, s, flag)
-                pack(0, x, s, h, [A[0, p, x + 1, part, :] for p in FACE[2][s]] + [flag])
-        return carry
-
-    lax.fori_loop(0, WX, first_stage, 0)
-    stage_rest(0, True, 0)
+                        stage_row(0, x, q, s, A[0, p, x + 1, part, :])
+                    stage_row(0, x, NQ, s, flag)
+                i = s * H + h
+                packed[i] = pack(packed[i], s, [A[0, p, x + 1, part, :] for p in FACE[2][s]] + [flag])
+        return tuple(packed)
+
+    packed = lax.fori_loop(0, WX, first_stage, blank)
+    stage_rest(0, True, 0, packed)
     send(0, True)
+    clear_missing()
     for c in copies[3:]:
         c.wait()
+    wait_send(0, True)
     wait_recv(0, True)
     merge(0, True, 0)
 
     def flags_z(x, carry):
-        for s in (0, 1):
-            for start in (Y0 - 8, Y0, Y0 + 8, Y0 + WY):
-                part = pl.ds(start, 8)
-                S[1 + s, x, part, :] = along_z(S[0, x, part, :], s, NQ, x, start)
+        for start in range(0, WY + 16, 8):
+            part = pl.ds(start, 8)
+            flag = S[0, x, part, :]
+            S[1, x, part, :] = pltpu.roll(flag, D - 1, 1)
+            S[2, x, part, :] = pltpu.roll(flag, 1, 1)
         return carry
 
     lax.fori_loop(0, WX + 2, flags_z, 0)
@@ -341,7 +367,7 @@
                 return here
             if c[2]:
                 s = side(c[2])
-                here = along_z(here, s, FACE[2][s].index(p), x + 1 + c[0], start + c[1])
+                here = pltpu.roll(here, D - 1 if s == 0 else 1, 1)
                 flag = S[1 + s, x + 1 + c[0], pl.ds(start + c[1], 8), :]
             else:
                 flag = S[0, x + 1 + c[0], pl.ds(start + c[1], 8), :]
@@ -408,7 +434,8 @@
         cur = lax.rem(k, 2)
         nxt = 1 - cur
 
-        def body(x, carry):
+        def body(x, packed):
+            packed = list(packed)
             for h, new in slab(k, cur, x):
                 part = pl.ds(Y0 + 8 * h, 8)
                 for p in range(NP):
@@ -416,13 +443,15 @@
                 for s in (0, 1):
                     if h == (0 if s == 0 else H - 1):
                         for q, p in enumerate(FACE[1][s]):
-                            stage_rows(k + 1, x, q, s, new[p])
-                    pack(k + 1, x, s, h, [new[p] for p in FACE[2][s]])
-            return carry
-
-        lax.fori_loop(0, WX, body, 0)
-        stage_rest(k + 1, False, nxt)
+                            stage_row(k + 1, x, q, s, new[p])
+                    i = s * H + h
+                    packed[i] = pack(packed[i], s, [new[p] for p in FACE[2][s]])
+            return tuple(packed)
+
+        packed = lax.fori_loop(0, WX, body, blank)
+        stage_rest(k + 1, False, nxt, packed)
         send(k + 1, False)
+        wait_send(k + 1, False)
         wait_recv(k + 1, False)
         merge(k + 1, False, nxt)
         return carry
@@ -443,8 +472,6 @@
         return carry
 
     lax.fori_loop(0, WX, last, 0)
-    for s in range(steps):
-        wait_send(s, s == 0)
 
 
 def solution(mesh):
@@ -470,18 +497,17 @@
             scratch_shapes=[
                 V((2, NP, WX + 2, WY + 16, D), f32),
                 V((3, WX + 2, WY + 16, D), f32),
-                V((2, WY + 16, D), f32),
                 V(rho.shape, rho.dtype),
                 V(vel.shape, vel.dtype),
                 V(lev.shape, lev.dtype),
                 V(solid.shape, solid.dtype),
                 V((steps, 2, NQ + 1, WY, D), f32),
-                V((steps, 2, NQ + 1, WX, 1, D), f32),
+                V((steps, 2, NQ + 1, WX, D), f32),
                 V((steps, 2, WY, D), f32),
                 V((steps, 4, 2, 1, D), f32),
                 V((steps, 4, 1, D), f32),
                 V((steps, 2, NQ + 1, WY, D), f32),
-                V((steps, 2, NQ + 1, WX, 1, D), f32),
+                V((steps, 2, NQ + 1, WX, D), f32),
                 V((steps, 2, WY, D), f32),
                 V((steps, 4, 2, 1, D), f32),
                 V((steps, 4, WY, D), f32),

time: 59.4 us -> 58.9 us (level)
  no operation moved by 1% of the time
where the time goes in v2:
time: 58.9 us; the launch traced here: 58.8 us
  Pallas kernels  53.8 us (91%)
  local copies, waits for them, and re-layouts  4.38 us (7%)
  between operations  0.65 us (1%)
    pallas_call x1, Pallas kernels, per_device(): pl.pallas_call(functools.partial(kernel, sizes, steps), out_shape=(jax.Sh...  53.8 us
    unnamed x4, local copies, waits for them, and re-layouts  4.38 us

profile of v2, /device:TPU:88, one launch (start us, length us, event | category | flops | bytes accessed | tf_op | source)
XLA Modules:
  0.0 58.8 jit_solution(3422147965540640593)
XLA Ops:
  0.6 53.8 %shard_map.86 = (f32[19,16,16,128]{3,2,1,0:T(8,128)}, f32[7,16,16,128]{3,2,1,0:T(8,128)}) custom-call(s32[64]{0:T(128)} %owner_ref.1, f32[19,16,16,128]{3,2,1,0:T(8,128)} %flow_hbm.1, f32[7,16,16,128]{3,2,1,0:T(8,128)} %sol_hbm.1, bf16[4,16,16,128]{3,2,1,0:T(8,128)(2,1)} %rho_hbm.1, bf16[4,3,16,16,128]{4,3,2,1,0:T(8,128)(2,1)} %vel_hbm.1, ...), custom_call_target="tpu_custom_call" | custom-call | tf_op jit(solution)/shard_map/pallas_call | solution.py:489
  54.4 0.0 copy-start
  54.4 3.4 %copy.11 = f32[19,16,16,128]{3,2,1,0:T(8,128)} copy(f32[19,16,16,128]{3,2,1,0:T(8,128)} %get-tuple-element.4) | data formatting | bytes 4980736
  57.9 0.0 copy-done
  57.9 0.9 %copy.12 = f32[7,16,16,128]{3,2,1,0:T(8,128)} copy(f32[7,16,16,128]{3,2,1,0:T(8,128)S(1)} %copy-done) | data formatting | bytes 1835008
Async XLA Ops:
  54.4 3.5 %copy-start = (f32[7,16,16,128]{3,2,1,0:T(8,128)S(1)}, f32[7,16,16,128]{3,2,1,0:T(8,128)}, u32[]{:S(2)}) copy-start(f32[7,16,16,128]{3,2,1,0:T(8,128)} %get-tuple-element.5) | copy-start | bytes 2752516

commit v3 on v2

v3 whole, which is shorter than its diff:
```python
import functools

import jax
import jax.numpy as jnp
from jax import lax
from jax.experimental import pallas as pl
from jax.experimental.pallas import tpu as pltpu
from jax.sharding import PartitionSpec as P

MESH = pl.DeviceIdType.MESH
BZC = 16

FLOW_DIRS = [
    (0, 0, 0),
    (1, 0, 0),
    (-1, 0, 0),
    (0, 1, 0),
    (0, -1, 0),
    (0, 0, 1),
    (0, 0, -1),
    (1, 1, 0),
    (-1, -1, 0),
    (1, -1, 0),
    (-1, 1, 0),
    (1, 0, 1),
    (-1, 0, -1),
    (1, 0, -1),
    (-1, 0, 1),
    (0, 1, 1),
    (0, -1, -1),
    (0, 1, -1),
    (0, -1, 1),
]
NF = 19
NP = NF + 7
OPP = [FLOW_DIRS.index((-c[0], -c[1], -c[2])) for c in FLOW_DIRS]
flow_omega = 1.25
solute_omega = 1.6
langmuir_rate = 0.05

FACE = [[[p for p in range(NF) if FLOW_DIRS[p][a] == s] for s in (1, -1)] for a in range(3)]
NQ = 5
SPAN = 18
FACES = FLOW_DIRS[1:7]
NBR = [c for c in FLOW_DIRS[1:] if c[2] and c[0]]
NBR += [c for c in FLOW_DIRS[1:] if c[2] and c[1]]
NBR += [c for c in FLOW_DIRS[1:] if c[2] and not c[0] and not c[1]]
NBR += [c for c in FLOW_DIRS[1:] if not c[2] and not (c[0] and c[1])]
NBR += [c for c in FLOW_DIRS[1:] if c[0] and c[1]]
XY = [c for c in NBR if c[0] and c[1]]
XZ = [c for c in NBR if c[0] and c[2]]
YZ = [c for c in NBR if c[1] and c[2]]
Y0 = 8


def side(step):
    return 0 if step > 0 else 1


def axis(c):
    return [i for i in range(3) if c[i]][0]


def neg(c):
    return (-c[0], -c[1], -c[2])


def kernel(
    sizes,
    steps,
    owner_ref,
    flow_hbm,
    sol_hbm,
    rho_hbm,
    vel_hbm,
    lev_hbm,
    solid_hbm,
    oflow,
    osol,
    A,
    B,
    S,
    Zf,
    ZR,
    PU,
    rho,
    vel,
    lev,
    solid,
    sx,
    sy,
    sz,
    sxy,
    sxz,
    syz,
    tx,
    ty,
    tz,
    rx,
    ry,
    rz,
    rxy,
    rxz,
    ryz,
    ux,
    uy,
    uz,
    in_sem,
    send_sem,
    recv_sem,
):
    WX, WY, D = solid.shape
    H = WY // 8
    names = ("gx", "gy", "gz")
    me = tuple(lax.axis_index(a) for a in names)

    inside = (pl.ds(1, WX), pl.ds(Y0, WY), slice(None))
    copies = [pltpu.make_async_copy(solid_hbm, solid, in_sem.at[0])]
    cuts = (0, 5, 10, 15, NF)
    for i, (lo, hi) in enumerate(zip(cuts, cuts[1:])):
        part = pl.ds(lo, hi - lo)
        copies.append(
            pltpu.make_async_copy(flow_hbm.at[part], A.at[(0, part) + inside], in_sem.at[1 + i])
        )
    copies.append(pltpu.make_async_copy(sol_hbm, B.at[(0, slice(None)) + inside], in_sem.at[5]))
    copies.append(pltpu.make_async_copy(lev_hbm, lev, in_sem.at[6]))
    copies.append(pltpu.make_async_copy(vel_hbm, vel, in_sem.at[7]))
    copies.append(pltpu.make_async_copy(rho_hbm, rho, in_sem.at[8]))
    for c in copies:
        c.start()

    def exists(c):
        ok = None
        for a in range(3):
            if c[a] > 0:
                t = me[a] < sizes[a] - 1
            elif c[a] < 0:
                t = me[a] > 0
            else:
                continue
            ok = t if ok is None else jnp.logical_and(ok, t)
        return ok

    def device(c):
        return tuple(me[a] + c[a] for a in range(3))

    barrier = pltpu.get_barrier_semaphore()
    for c in NBR:

        @pl.when(exists(c))
        def _(c=c):
            pl.semaphore_signal(barrier, inc=1, device_id=device(c), device_id_type=MESH)

    count = jnp.int32(0)
    for i in range(owner_ref.shape[0]):
        count = count + (owner_ref[i] == me[2]).astype(jnp.int32)
    top = count * BZC - 1

    lane = lax.broadcasted_iota(jnp.int32, (8, D), 1)
    row = lax.broadcasted_iota(jnp.int32, (8, D), 0)
    edge = (lane == top, lane == 0)
    last_column = SPAN - 2
    slot_lane = (lane - last_column, (lane - (top + last_column) + 2 * D) % D)

    n = [
        (me[a] > 0).astype(jnp.int32) + (me[a] < sizes[a] - 1).astype(jnp.int32) for a in range(3)
    ]
    pl.semaphore_wait(
        barrier, n[0] + n[1] + n[2] + n[0] * n[1] + n[0] * n[2] + n[1] * n[2]
    )

    def flow_refs(c, slot, first):
        nq = NQ + 1 if first else NQ
        if c in XY:
            part = (slot, XY.index(c), pl.ds(0, nq - NQ + 1))
            return sxy.at[part], rxy.at[part]
        if c in XZ:
            part = (slot, XZ.index(c))
            return sxz.at[part], rxz.at[part]
        if c in YZ:
            part = (slot, YZ.index(c))
            return syz.at[part], ryz.at[part]
        a = axis(c)
        part = (slot, side(c[a]))
        if a == 2:
            return sz.at[part], rz.at[part]
        part = part + (pl.ds(0, nq),)
        return ((sx, rx), (sy, ry))[a][0].at[part], ((sx, rx), (sy, ry))[a][1].at[part]

    def flow_message(c, slot, first):
        src, dst = flow_refs(c, slot, first)
        i = NBR.index(c)
        return pltpu.make_async_remote_copy(
            src_ref=src,
            dst_ref=dst,
            send_sem=send_sem.at[slot, i],
            recv_sem=recv_sem.at[slot, i],
            device_id=device(neg(c)),
            device_id_type=MESH,
        )

    def sol_message(c, slot):
        a = axis(c)
        part = (slot, side(c[a]))
        i = len(NBR) + FACES.index(c)
        return pltpu.make_async_remote_copy(
            src_ref=(tx, ty, tz)[a].at[part],
            dst_ref=(ux, uy, uz)[a].at[part],
            send_sem=send_sem.at[slot, i],
            recv_sem=recv_sem.at[slot, i],
            device_id=device(neg(c)),
            device_id_type=MESH,
        )

    def each(table, there, act):
        for c in table:

            @pl.when(exists(there(c)))
            def _(c=c):
                act(c)

    same = lambda c: c

    def send_flow(slot, first):
        each(NBR, neg, lambda c: flow_message(c, slot, first).start())

    def wait_flow(slot, first):
        each(NBR, neg, lambda c: flow_message(c, slot, first).wait_send())
        each(NBR, same, lambda c: flow_message(c, slot, first).wait_recv())

    def send_sol(slot):
        each(FACES, neg, lambda c: sol_message(c, slot).start())

    def wait_sol(slot):
        each(FACES, neg, lambda c: sol_message(c, slot).wait_send())
        each(FACES, same, lambda c: sol_message(c, slot).wait_recv())

    def clear_missing():
        for c in NBR:

            @pl.when(jnp.logical_not(exists(c)))
            def _(c=c):
                for k in range(2):
                    refs = [flow_refs(c, k, True)[1]]
                    if c in FACES:
                        refs.append((ux, uy, uz)[axis(c)].at[k, side(c[axis(c)])])
                    for ref in refs:
                        ref[...] = jnp.zeros(ref.shape, ref.dtype)

    def edge_row(value, s):
        return value[0:1] if s == 0 else value[7:8]

    def pack(acc, s, values):
        acc = pltpu.roll(acc, D - 1, 1)
        for q, value in enumerate(values):
            moved = pltpu.roll(value, q * SPAN + last_column, 1)
            acc = jnp.where(slot_lane[s] == q * SPAN, moved, acc)
        return acc

    def settle(face, s):
        return face if s == 0 else pltpu.roll(face, D - top, 1)

    def stage_flow(slot, first, cur, packed):
        for s in (0, 1):
            face = [settle(packed[s * H + h], s) for h in range(H)]
            for h in range(H):
                sz[slot, s, pl.ds(8 * h, 8), :] = face[h]
            for d, c in enumerate(YZ):
                if side(c[2]) == s:
                    syz[slot, d] = face[0][0:1] if c[1] > 0 else face[H - 1][7:8]
            for d, c in enumerate(XZ):
                if side(c[2]) == s:
                    column = 1 if c[0] > 0 else WX
                    q = FACE[2][s].index(FLOW_DIRS.index(c))
                    line = jnp.zeros((8, D), jnp.float32)
                    for at, qz in enumerate((q, NQ) if first else (q,)):
                        i = qz * SPAN + column
                        for h in range(H):
                            value = jnp.broadcast_to(face[h][:, i : i + 1], (8, D))
                            line = jnp.where(lane == row + (WY * at + 8 * h), value, line)
                    sxz[slot, d] = jnp.sum(line, axis=0, keepdims=True)
        for s in (0, 1):
            x = 1 if s == 0 else WX
            for q, p in enumerate(FACE[0][s]):
                sx[slot, s, q] = A[cur, p, x, pl.ds(Y0, WY), :]
            if first:
                sx[slot, s, NQ] = S[0, x, pl.ds(Y0, WY), :]
        for d, c in enumerate(XY):
            q = FACE[1][side(c[1])].index(FLOW_DIRS.index(c))
            x = 0 if c[0] > 0 else WX - 1
            sxy[slot, d, 0] = sy[slot, side(c[1]), q, pl.ds(x, 1), :]
            if first:
                sxy[slot, d, 1] = sy[slot, side(c[1]), NQ, pl.ds(x, 1), :]

    def column_of(line, start):
        line = jnp.broadcast_to(line, (8, D))
        return jnp.sum(jnp.where(lane == row + start, line, 0.0), axis=1, keepdims=True)

    def merge_flow(slot, first, cur):
        flag = [(NQ, None)] if first else []

        def put(p, x, rows, value):
            if p is None:
                S[0, x, rows, :] = value
            else:
                A[cur, p, x, rows, :] = value

        for s in (0, 1):
            x = WX + 1 if s == 0 else 0
            for q, p in list(enumerate(FACE[0][s])) + flag:
                put(p, x, pl.ds(Y0, WY), rx[slot, s, q])
            y = Y0 + WY if s == 0 else Y0 - 1
            for q, p in list(enumerate(FACE[1][s])) + flag:
                for half in range(WX // 8):
                    value = ry[slot, s, q, pl.ds(8 * half, 8), :]
                    for i in range(8):
                        put(p, 1 + 8 * half + i, pl.ds(y, 1), value[i : i + 1])
        for d, c in enumerate(XY):
            x = WX + 1 if c[0] > 0 else 0
            y = Y0 + WY if c[1] > 0 else Y0 - 1
            put(FLOW_DIRS.index(c), x, pl.ds(y, 1), rxy[slot, d, 0])
            if first:
                put(None, x, pl.ds(y, 1), rxy[slot, d, 1])
        for s in (0, 1):
            cz = 1 - 2 * s
            turn = (lambda v: pltpu.roll(v, top, 1)) if s == 0 else (lambda v: v)
            for h in range(H):
                face = rz[slot, s, pl.ds(8 * h, 8), :]
                for cx in (1, -1):
                    c = (cx, 0, cz)
                    q = FACE[2][s].index(FLOW_DIRS.index(c))
                    for at, qz in enumerate((q, NQ) if first else (q,)):
                        value = column_of(rxz[slot, XZ.index(c)], WY * at + 8 * h)
                        i = qz * SPAN + (WX + 1 if cx > 0 else 0)
                        face = jnp.where(lane == i, value, face)
                Zf[s, pl.ds(Y0 + 8 * h, 8), :] = turn(face)
            for y, cy in ((Y0 + WY, 1), (Y0 - 1, -1)):
                line = jnp.broadcast_to(ryz[slot, YZ.index((0, cy, cz))], (8, D))
                Zf[s, pl.ds(y, 1), :] = turn(line)[0:1]
            for t in range(3):
                face = Zf[s, pl.ds(Y0 - 1 + 8 * t, 8), :]
                for x in range(WX):
                    ZR[s, x, pl.ds(8 * t, 8), :] = pltpu.roll(face, D - x, 1) if x else face

    for c in copies[:6]:
        c.wait()

    zero = jnp.zeros((8, D), jnp.float32)
    for s in (0, 1):
        for part in range(0, WY + 16, 8):
            Zf[s, pl.ds(part, 8), :] = zero
    for part in (0, Y0 + WY):
        for x in range(WX + 2):
            S[0, x, pl.ds(part, 8), :] = zero

    blank = (zero,) * (2 * H)

    def stage_tile(slot, x, h, values, packed, flag=None):
        extra = [] if flag is None else [flag]
        for s in (0, 1):
            if h == (0 if s == 0 else H - 1):
                for q, value in enumerate([values[p] for p in FACE[1][s]] + extra):
                    sy[slot, s, q, pl.ds(x, 1), :] = edge_row(value, s)
            i = s * H + h
            packed[i] = pack(packed[i], s, [values[p] for p in FACE[2][s]] + extra)

    def stage_sol_tile(slot, x, h, values, packed):
        for s in (0, 1):
            if h == (0 if s == 0 else H - 1):
                ty[slot, s, pl.ds(x, 1), :] = edge_row(values[3 + s], s)
            i = s * H + h
            packed[i] = pack(packed[i], s, [values[5 + s]])

    def stage_sol(slot, cur, packed):
        for s in (0, 1):
            for h in range(H):
                tz[slot, s, pl.ds(8 * h, 8), :] = settle(packed[s * H + h], s)
            tx[slot, s] = B[cur, 1 + s, 1 if s == 0 else WX, pl.ds(Y0, WY), :]

    class Tiles:
        def __init__(self, ref, x, part):
            self.ref, self.x, self.part = ref, x, part

        def __getitem__(self, p):
            return self.ref[0, p, self.x + 1, self.part, :]

    def first_stage(x, packed):
        packed, other = list(packed[0]), list(packed[1])
        flags = solid[x].astype(jnp.float32)
        S[0, x + 1, pl.ds(Y0, WY), :] = flags
        for h in range(H):
            part = pl.ds(Y0 + 8 * h, 8)
            stage_tile(0, x, h, Tiles(A, x, part), packed, flags[8 * h : 8 * h + 8])
            stage_sol_tile(0, x, h, Tiles(B, x, part), other)
        return tuple(packed), tuple(other)

    packed, other = lax.fori_loop(0, WX, first_stage, (blank, blank))
    stage_flow(0, True, 0, packed)
    send_flow(0, True)
    stage_sol(0, 0, other)
    send_sol(0)
    clear_missing()
    for c in copies[6:]:
        c.wait()
    wait_flow(0, True)
    merge_flow(0, True, 0)
    for x in range(WX + 2):
        for t in range(0, WY + 16, 8):
            part = pl.ds(t, 8)
            flag = S[0, x, part, :]
            for s in (0, 1):
                halo = pltpu.roll(Zf[s, part, :], D - (NQ * SPAN + x), 1)
                moved = pltpu.roll(flag, D - 1 if s == 0 else 1, 1)
                S[1 + s, x, part, :] = jnp.where(edge[s], halo, moved)

    def solute_step(j, slot):
        t = steps - 1 - j
        cur = slot
        nxt = 1 - slot
        wait_sol(slot)
        for s in (0, 1):
            B[cur, 1 + s, WX + 1 if s == 0 else 0, pl.ds(Y0, WY), :] = ux[slot, s]
            y = Y0 + WY if s == 0 else Y0 - 1
            for half in range(WX // 8):
                value = uy[slot, s, pl.ds(8 * half, 8), :]
                for i in range(8):
                    B[cur, 3 + s, 1 + 8 * half + i, pl.ds(y, 1), :] = value[i : i + 1]
        halo = []
        for s in (0, 1):
            for h in range(H):
                face = uz[slot, s, pl.ds(8 * h, 8), :]
                halo.append(pltpu.roll(face, top - 1 if s == 0 else D - 1, 1))

        def body(x, carry):
            halo, packed = list(carry[0]), list(carry[1])
            level_ = lev[t, x].astype(jnp.float32)
            density_ = rho[t, x].astype(jnp.float32)
            u_ = [vel[t, i, x].astype(jnp.float32) for i in range(3)]
            for h in range(H):
                cut = slice(8 * h, 8 * h + 8)
                level, density, u = level_[cut], density_[cut], [v[cut] for v in u_]
                start = Y0 + 8 * h
                here = pl.ds(start, 8)
                hs = [B[cur, 0, x + 1, here, :]]
                for p in range(1, 7):
                    c = FLOW_DIRS[p]
                    rows = pl.ds(start + c[1], 8)
                    value = B[cur, p, x + 1 + c[0], rows, :]
                    if c[2]:
                        s = side(c[2])
                        value = pltpu.roll(value, D - 1 if s == 0 else 1, 1)
                        value = jnp.where(edge[s], halo[s * H + h], value)
                        flag = S[1 + s, x + 1, here, :]
                    else:
                        flag = S[0, x + 1 + c[0], rows, :]
                    hs.append(jnp.where(flag > 0.5, B[cur, OPP[p], x + 1, here, :], value))
                mx, my, mz = hs[1] - hs[2], hs[3] - hs[4], hs[5] - hs[6]
                m0 = 0.25 * hs[0] + 0.125 * ((hs[1] + hs[2]) + (hs[3] + hs[4]) + (hs[5] + hs[6]))
                along = mx * u[0] + my * u[1] + mz * u[2]
                one = 1.0 + level
                common = (solute_omega - langmuir_rate / (one * one)) * m0 + (
                    solute_omega * 0.5
                ) * along
                new = [(1.0 - solute_omega) * v + common for v in hs]
                for p in range(7):
                    B[nxt, p, x + 1, here, :] = new[p]
                stage_sol_tile(nxt, x, h, new, packed)
                factor = (0.5 * solute_omega) * level * (1.0 / density)
                speed = u[0] * u[0] + u[1] * u[1] + u[2] * u[2]
                saved = [factor * mx, factor * my, factor * mz, factor * along]
                for i, v in enumerate(saved + u + [1.0 + 1.5 * speed]):
                    PU[i, x, pl.ds(8 * h, 8), :] = v
            return tuple(pltpu.roll(v, D - 1, 1) for v in halo), tuple(packed)

        _, packed = lax.fori_loop(0, WX, body, (tuple(halo), blank))
        stage_sol(nxt, nxt, packed)

    def flow_tile(cur, x, h):
        start = Y0 + 8 * h

        def read(p):
            c = FLOW_DIRS[p]
            rows = pl.ds(start + c[1], 8)
            here = A[cur, p, x + 1 + c[0], rows, :]
            if c == (0, 0, 0):
                return here
            if c[2]:
                s = side(c[2])
                here = pltpu.roll(here, D - 1 if s == 0 else 1, 1)
                lift = FACE[2][s].index(p) * SPAN + 1 + c[0]
                halo = ZR[s, x, pl.ds(8 * h + 1 + c[1], 8), :]
                halo = pltpu.roll(halo, D - lift, 1) if lift else halo
                here = jnp.where(edge[s], halo, here)
                flag = S[1 + s, x + 1 + c[0], rows, :]
            else:
                flag = S[0, x + 1 + c[0], rows, :]
            back = A[cur, OPP[p], x + 1, pl.ds(start, 8), :]
            return jnp.where(flag > 0.5, back, here)

        part = pl.ds(8 * h, 8)
        px, py, pz, along, ux, uy, uz, stretch = [PU[i, x, part, :] for i in range(8)]
        g = [read(p) for p in range(NF)]
        a = [g[p] + g[p + 1] for p in range(1, NF, 2)]
        d = [g[p] - g[p + 1] for p in range(1, NF, 2)]
        ax, ay, az = 2.0 * a[0], 2.0 * a[1], 2.0 * a[2]
        sxy_, sxz_, syz_ = a[3] + a[4], a[5] + a[6], a[7] + a[8]
        qxy, qxz, qyz = a[3] - a[4], a[5] - a[6], a[7] - a[8]
        qxx, qyy, qzz = ax + sxy_ + sxz_, ay + sxy_ + syz_, az + sxz_ + syz_
        total = 12.0 * g[0] + (qxx + ay + az) + syz_
        jx = 2.0 * d[0] + (d[3] + d[4]) + (d[5] + d[6])
        jy = 2.0 * d[1] + (d[3] - d[4]) + (d[7] + d[8])
        jz = 2.0 * d[2] + (d[5] - d[6]) + (d[7] - d[8])
        vx = qxx * ux + qxy * uy + qxz * uz
        vy = qxy * ux + qyy * uy + qyz * uz
        vz = qxz * ux + qyz * uy + qzz * uz
        quad = vx * ux + vy * uy + vz * uz
        w = flow_omega / 36.0
        scalar = w * (total * stretch - 4.5 * quad) - along
        tx_ = (3.0 * w) * (jx + 3.0 * vx - ux * total) + px
        ty_ = (3.0 * w) * (jy + 3.0 * vy - uy * total) + py
        tz_ = (3.0 * w) * (jz + 3.0 * vz - uz * total) + pz
        rest = 1.0 - flow_omega
        new = [rest * g[0] + scalar]
        pairs = [tx_, ty_, tz_, tx_ + ty_, tx_ - ty_, tx_ + tz_, tx_ - tz_, ty_ + tz_, ty_ - tz_]
        for i, v in enumerate(pairs):
            p = 1 + 2 * i
            new.append(rest * g[p] + (scalar + v))
            new.append(rest * g[p + 1] + (scalar - v))
        return new

    solute_step(0, 0)
    send_sol(1)

    def step(k, carry):
        cur = lax.rem(k, 2)
        nxt = 1 - cur

        def body(x, packed):
            packed = list(packed)
            for h in range(H):
                new = flow_tile(cur, x, h)
                for p in range(NF):
                    A[nxt, p, x + 1, pl.ds(Y0 + 8 * h, 8), :] = new[p]
                stage_tile(nxt, x, h, new, packed)
            return tuple(packed)

        packed = lax.fori_loop(0, WX, body, blank)
        stage_flow(nxt, False, nxt, packed)
        send_flow(nxt, False)
        solute_step(k + 1, nxt)

        @pl.when(k < steps - 2)
        def _():
            send_sol(cur)

        wait_flow(nxt, False)
        merge_flow(nxt, False, nxt)
        return carry

    lax.fori_loop(0, steps - 1, step, 0)

    def last(x, carry):
        for h in range(H):
            new = flow_tile((steps - 1) % 2, x, h)
            part = pl.ds(8 * h, 8)
            here = pl.ds(Y0 + 8 * h, 8)
            keep = (S[0, x + 1, here, :] < 0.5) & (lane <= top)
            for p in range(NF):
                oflow[p, x, part, :] = jnp.where(keep, new[p], 0.0)
            for p in range(NP - NF):
                osol[p, x, part, :] = jnp.where(keep, B[steps % 2, p, x + 1, here, :], 0.0)
        return carry

    lax.fori_loop(0, WX, last, 0)


def solution(mesh):
    names = ("gx", "gy", "gz")
    sizes = tuple(mesh.shape[a] for a in names)

    def per_device(flow, solute, rho, vel, lev, solid, owner):
        WX, WY, D = solid.shape
        steps = rho.shape[0]
        f32 = jnp.float32
        V = pltpu.VMEM
        DMA = pltpu.SemaphoreType.DMA
        hbm = pl.BlockSpec(memory_space=pl.ANY)
        n = len(NBR) + len(FACES)
        faces = [
            V((2, 2, NQ + 1, WY, D), f32),
            V((2, 2, NQ + 1, WX, D), f32),
            V((2, 2, WY, D), f32),
            V((2, 4, 2, 1, D), f32),
            V((2, 4, 1, D), f32),
            V((2, 4, 1, D), f32),
        ]
        sides = [V((2, 2, WY, D), f32), V((2, 2, WX, D), f32), V((2, 2, WY, D), f32)]
        return pl.pallas_call(
            functools.partial(kernel, sizes, steps),
            out_shape=(
                jax.ShapeDtypeStruct(flow.shape, f32),
                jax.ShapeDtypeStruct(solute.shape, f32),
            ),
            in_specs=[pl.BlockSpec(memory_space=pltpu.SMEM)] + [hbm] * 6,
            out_specs=(pl.BlockSpec(memory_space=pltpu.VMEM),) * 2,
            scratch_shapes=[
                V((2, NF, WX + 2, WY + 16, D), f32),
                V((2, NP - NF, WX + 2, WY + 16, D), f32),
                V((3, WX + 2, WY + 16, D), f32),
                V((2, WY + 16, D), f32),
                V((2, WX, WY + 8, D), f32),
                V((8, WX, WY, D), f32),
                V(rho.shape, rho.dtype),
                V(vel.shape, vel.dtype),
                V(lev.shape, lev.dtype),
                V(solid.shape, solid.dtype),
            ]
            + (faces + sides) * 2
            + [DMA((9,)), DMA((2, n)), DMA((2, n))],
            compiler_params=pltpu.CompilerParams(
                collective_id=0, has_side_effects=True, vmem_limit_bytes=60 * 2**20
            ),
        )(owner, flow, solute, rho, vel, lev, solid)

    field = P(None, "gx", "gy", "gz")
    return jax.shard_map(
        per_device,
        mesh=mesh,
        in_specs=(field, field, field, P(None, None, "gx", "gy", "gz"), field, P("gx", "gy", "gz"), P()),
        out_specs=(field, field),
        check_vma=False,
    )
```

time: 58.9 us -> 58.4 us (level)
  Pallas kernels: 53.8 us -> 53.2 us
where the time goes in v3:
time: 58.4 us; the launch traced here: 58.3 us
  Pallas kernels  53.2 us (91%)
  local copies, waits for them, and re-layouts  4.38 us (8%)
  between operations  0.65 us (1%)
    pallas_call x1, Pallas kernels, per_device(): pl.pallas_call(functools.partial(kernel, sizes, steps), out_shape=(jax.Sh...  53.2 us
    unnamed x4, local copies, waits for them, and re-layouts  4.38 us

profile of v3, /device:TPU:88, one launch (start us, length us, event | category | flops | bytes accessed | tf_op | source)
XLA Modules:
  0.0 58.3 jit_solution(5275123566309413688)
XLA Ops:
  0.6 53.2 %shard_map.86 = (f32[19,16,16,128]{3,2,1,0:T(8,128)}, f32[7,16,16,128]{3,2,1,0:T(8,128)}) custom-call(s32[64]{0:T(128)} %owner_ref.1, f32[19,16,16,128]{3,2,1,0:T(8,128)} %flow_hbm.1, f32[7,16,16,128]{3,2,1,0:T(8,128)} %sol_hbm.1, bf16[4,16,16,128]{3,2,1,0:T(8,128)(2,1)} %rho_hbm.1, bf16[4,3,16,16,128]{4,3,2,1,0:T(8,128)(2,1)} %vel_hbm.1, ...), custom_call_target="tpu_custom_call" | custom-call | tf_op jit(solution)/shard_map/pallas_call | solution.py:598
  53.9 0.0 copy-start
  53.9 3.4 %copy.11 = f32[19,16,16,128]{3,2,1,0:T(8,128)} copy(f32[19,16,16,128]{3,2,1,0:T(8,128)} %get-tuple-element.4) | data formatting | bytes 4980736
  57.3 0.0 copy-done
  57.3 0.9 %copy.12 = f32[7,16,16,128]{3,2,1,0:T(8,128)} copy(f32[7,16,16,128]{3,2,1,0:T(8,128)S(1)} %copy-done) | data formatting | bytes 1835008
Async XLA Ops:
  53.9 3.5 %copy-start = (f32[7,16,16,128]{3,2,1,0:T(8,128)S(1)}, f32[7,16,16,128]{3,2,1,0:T(8,128)}, u32[]{:S(2)}) copy-start(f32[7,16,16,128]{3,2,1,0:T(8,128)} %get-tuple-element.5) | copy-start | bytes 2752516

commit v4 on v3

--- a/solution.py
+++ b/solution.py
@@ -50,6 +50,9 @@
 XY = [c for c in NBR if c[0] and c[1]]
 XZ = [c for c in NBR if c[0] and c[2]]
 YZ = [c for c in NBR if c[1] and c[2]]
+FLAT = [c for c in NBR if not c[2]]
+UPDOWN = [c for c in NBR if c[2]]
+U_FLOW, U_SOL = 2, 4
 Y0 = 8
 
 
@@ -77,8 +80,10 @@
     solid_hbm,
     oflow,
     osol,
-    A,
-    B,
+    A0,
+    A1,
+    B0,
+    B1,
     S,
     Zf,
     ZR,
@@ -111,6 +116,7 @@
 ):
     WX, WY, D = solid.shape
     H = WY // 8
+    A, B = (A0, A1), (B0, B1)
     names = ("gx", "gy", "gz")
     me = tuple(lax.axis_index(a) for a in names)
 
@@ -120,9 +126,9 @@
     for i, (lo, hi) in enumerate(zip(cuts, cuts[1:])):
         part = pl.ds(lo, hi - lo)
         copies.append(
-            pltpu.make_async_copy(flow_hbm.at[part], A.at[(0, part) + inside], in_sem.at[1 + i])
+            pltpu.make_async_copy(flow_hbm.at[part], A0.at[(part,) + inside], in_sem.at[1 + i])
         )
-    copies.append(pltpu.make_async_copy(sol_hbm, B.at[(0, slice(None)) + inside], in_sem.at[5]))
+    copies.append(pltpu.make_async_copy(sol_hbm, B0.at[(slice(None),) + inside], in_sem.at[5]))
     copies.append(pltpu.make_async_copy(lev_hbm, lev, in_sem.at[6]))
     copies.append(pltpu.make_async_copy(vel_hbm, vel, in_sem.at[7]))
     copies.append(pltpu.make_async_copy(rho_hbm, rho, in_sem.at[8]))
@@ -226,7 +232,10 @@
 
     def wait_flow(slot, first):
         each(NBR, neg, lambda c: flow_message(c, slot, first).wait_send())
-        each(NBR, same, lambda c: flow_message(c, slot, first).wait_recv())
+        each(FLAT, same, lambda c: flow_message(c, slot, first).wait_recv())
+        merge_flat(slot, first, slot)
+        each(UPDOWN, same, lambda c: flow_message(c, slot, first).wait_recv())
+        merge_z(slot, first)
 
     def send_sol(slot):
         each(FACES, neg, lambda c: sol_message(c, slot).start())
@@ -246,6 +255,14 @@
                         refs.append((ux, uy, uz)[axis(c)].at[k, side(c[axis(c)])])
                     for ref in refs:
                         ref[...] = jnp.zeros(ref.shape, ref.dtype)
+
+    def over_x(body, init, unroll):
+        def trip(i, carry):
+            for j in range(unroll):
+                carry = body(unroll * i + j, carry)
+            return carry
+
+        return lax.fori_loop(0, WX // unroll, trip, init)
 
     def edge_row(value, s):
         return value[0:1] if s == 0 else value[7:8]
@@ -282,7 +299,7 @@
         for s in (0, 1):
             x = 1 if s == 0 else WX
             for q, p in enumerate(FACE[0][s]):
-                sx[slot, s, q] = A[cur, p, x, pl.ds(Y0, WY), :]
+                sx[slot, s, q] = A[cur][p, x, pl.ds(Y0, WY), :]
             if first:
                 sx[slot, s, NQ] = S[0, x, pl.ds(Y0, WY), :]
         for d, c in enumerate(XY):
@@ -296,14 +313,14 @@
         line = jnp.broadcast_to(line, (8, D))
         return jnp.sum(jnp.where(lane == row + start, line, 0.0), axis=1, keepdims=True)
 
-    def merge_flow(slot, first, cur):
+    def merge_flat(slot, first, cur):
         flag = [(NQ, None)] if first else []
 
         def put(p, x, rows, value):
             if p is None:
                 S[0, x, rows, :] = value
             else:
-                A[cur, p, x, rows, :] = value
+                A[cur][p, x, rows, :] = value
 
         for s in (0, 1):
             x = WX + 1 if s == 0 else 0
@@ -321,6 +338,8 @@
             put(FLOW_DIRS.index(c), x, pl.ds(y, 1), rxy[slot, d, 0])
             if first:
                 put(None, x, pl.ds(y, 1), rxy[slot, d, 1])
+
+    def merge_z(slot, first):
         for s in (0, 1):
             cz = 1 - 2 * s
             turn = (lambda v: pltpu.roll(v, top, 1)) if s == 0 else (lambda v: v)
@@ -375,14 +394,14 @@
         for s in (0, 1):
             for h in range(H):
                 tz[slot, s, pl.ds(8 * h, 8), :] = settle(packed[s * H + h], s)
-            tx[slot, s] = B[cur, 1 + s, 1 if s == 0 else WX, pl.ds(Y0, WY), :]
+            tx[slot, s] = B[cur][1 + s, 1 if s == 0 else WX, pl.ds(Y0, WY), :]
 
     class Tiles:
         def __init__(self, ref, x, part):
             self.ref, self.x, self.part = ref, x, part
 
         def __getitem__(self, p):
-            return self.ref[0, p, self.x + 1, self.part, :]
+            return self.ref[p, self.x + 1, self.part, :]
 
     def first_stage(x, packed):
         packed, other = list(packed[0]), list(packed[1])
@@ -390,11 +409,11 @@
         S[0, x + 1, pl.ds(Y0, WY), :] = flags
         for h in range(H):
             part = pl.ds(Y0 + 8 * h, 8)
-            stage_tile(0, x, h, Tiles(A, x, part), packed, flags[8 * h : 8 * h + 8])
-            stage_sol_tile(0, x, h, Tiles(B, x, part), other)
+            stage_tile(0, x, h, Tiles(A0, x, part), packed, flags[8 * h : 8 * h + 8])
+            stage_sol_tile(0, x, h, Tiles(B0, x, part), other)
         return tuple(packed), tuple(other)
 
-    packed, other = lax.fori_loop(0, WX, first_stage, (blank, blank))
+    packed, other = over_x(first_stage, (blank, blank), 2)
     stage_flow(0, True, 0, packed)
     send_flow(0, True)
     stage_sol(0, 0, other)
@@ -403,7 +422,6 @@
     for c in copies[6:]:
         c.wait()
     wait_flow(0, True)
-    merge_flow(0, True, 0)
     for x in range(WX + 2):
         for t in range(0, WY + 16, 8):
             part = pl.ds(t, 8)
@@ -419,12 +437,12 @@
         nxt = 1 - slot
         wait_sol(slot)
         for s in (0, 1):
-            B[cur, 1 + s, WX + 1 if s == 0 else 0, pl.ds(Y0, WY), :] = ux[slot, s]
+            B[cur][1 + s, WX + 1 if s == 0 else 0, pl.ds(Y0, WY), :] = ux[slot, s]
             y = Y0 + WY if s == 0 else Y0 - 1
             for half in range(WX // 8):
                 value = uy[slot, s, pl.ds(8 * half, 8), :]
                 for i in range(8):
-                    B[cur, 3 + s, 1 + 8 * half + i, pl.ds(y, 1), :] = value[i : i + 1]
+                    B[cur][3 + s, 1 + 8 * half + i, pl.ds(y, 1), :] = value[i : i + 1]
         halo = []
         for s in (0, 1):
             for h in range(H):
@@ -441,11 +459,11 @@
                 level, density, u = level_[cut], density_[cut], [v[cut] for v in u_]
                 start = Y0 + 8 * h
                 here = pl.ds(start, 8)
-                hs = [B[cur, 0, x + 1, here, :]]
+                hs = [B[cur][0, x + 1, here, :]]
                 for p in range(1, 7):
                     c = FLOW_DIRS[p]
                     rows = pl.ds(start + c[1], 8)
-                    value = B[cur, p, x + 1 + c[0], rows, :]
+                    value = B[cur][p, x + 1 + c[0], rows, :]
                     if c[2]:
                         s = side(c[2])
                         value = pltpu.roll(value, D - 1 if s == 0 else 1, 1)
@@ -453,7 +471,7 @@
                         flag = S[1 + s, x + 1, here, :]
                     else:
                         flag = S[0, x + 1 + c[0], rows, :]
-                    hs.append(jnp.where(flag > 0.5, B[cur, OPP[p], x + 1, here, :], value))
+                    hs.append(jnp.where(flag > 0.5, B[cur][OPP[p], x + 1, here, :], value))
                 mx, my, mz = hs[1] - hs[2], hs[3] - hs[4], hs[5] - hs[6]
                 m0 = 0.25 * hs[0] + 0.125 * ((hs[1] + hs[2]) + (hs[3] + hs[4]) + (hs[5] + hs[6]))
                 along = mx * u[0] + my * u[1] + mz * u[2]
@@ -463,7 +481,7 @@
                 ) * along
                 new = [(1.0 - solute_omega) * v + common for v in hs]
                 for p in range(7):
-                    B[nxt, p, x + 1, here, :] = new[p]
+                    B[nxt][p, x + 1, here, :] = new[p]
                 stage_sol_tile(nxt, x, h, new, packed)
                 factor = (0.5 * solute_omega) * level * (1.0 / density)
                 speed = u[0] * u[0] + u[1] * u[1] + u[2] * u[2]
@@ -472,7 +490,7 @@
                     PU[i, x, pl.ds(8 * h, 8), :] = v
             return tuple(pltpu.roll(v, D - 1, 1) for v in halo), tuple(packed)
 
-        _, packed = lax.fori_loop(0, WX, body, (tuple(halo), blank))
+        _, packed = over_x(body, (tuple(halo), blank), U_SOL)
         stage_sol(nxt, nxt, packed)
 
     def flow_tile(cur, x, h):
@@ -481,7 +499,7 @@
         def read(p):
             c = FLOW_DIRS[p]
             rows = pl.ds(start + c[1], 8)
-            here = A[cur, p, x + 1 + c[0], rows, :]
+            here = A[cur][p, x + 1 + c[0], rows, :]
             if c == (0, 0, 0):
                 return here
             if c[2]:
@@ -494,7 +512,7 @@
                 flag = S[1 + s, x + 1 + c[0], rows, :]
             else:
                 flag = S[0, x + 1 + c[0], rows, :]
-            back = A[cur, OPP[p], x + 1, pl.ds(start, 8), :]
+            back = A[cur][OPP[p], x + 1, pl.ds(start, 8), :]
             return jnp.where(flag > 0.5, back, here)
 
         part = pl.ds(8 * h, 8)
@@ -531,8 +549,8 @@
     solute_step(0, 0)
     send_sol(1)
 
-    def step(k, carry):
-        cur = lax.rem(k, 2)
+    def step(k):
+        cur = k % 2
         nxt = 1 - cur
 
         def body(x, packed):
@@ -540,24 +558,21 @@
             for h in range(H):
                 new = flow_tile(cur, x, h)
                 for p in range(NF):
-                    A[nxt, p, x + 1, pl.ds(Y0 + 8 * h, 8), :] = new[p]
+                    A[nxt][p, x + 1, pl.ds(Y0 + 8 * h, 8), :] = new[p]
                 stage_tile(nxt, x, h, new, packed)
             return tuple(packed)
 
-        packed = lax.fori_loop(0, WX, body, blank)
+        packed = over_x(body, blank, U_FLOW)
         stage_flow(nxt, False, nxt, packed)
         send_flow(nxt, False)
         solute_step(k + 1, nxt)
 
-        @pl.when(k < steps - 2)
-        def _():
+        if k < steps - 2:
             send_sol(cur)
-
         wait_flow(nxt, False)
-        merge_flow(nxt, False, nxt)
-        return carry
-
-    lax.fori_loop(0, steps - 1, step, 0)
+
+    for k in range(steps - 1):
+        step(k)
 
     def last(x, carry):
         for h in range(H):
@@ -568,10 +583,10 @@
             for p in range(NF):
                 oflow[p, x, part, :] = jnp.where(keep, new[p], 0.0)
             for p in range(NP - NF):
-                osol[p, x, part, :] = jnp.where(keep, B[steps % 2, p, x + 1, here, :], 0.0)
+                osol[p, x, part, :] = jnp.where(keep, B[steps % 2][p, x + 1, here, :], 0.0)
         return carry
 
-    lax.fori_loop(0, WX, last, 0)
+    over_x(last, 0, U_FLOW)
 
 
 def solution(mesh):
@@ -604,8 +619,10 @@
             in_specs=[pl.BlockSpec(memory_space=pltpu.SMEM)] + [hbm] * 6,
             out_specs=(pl.BlockSpec(memory_space=pltpu.VMEM),) * 2,
             scratch_shapes=[
-                V((2, NF, WX + 2, WY + 16, D), f32),
-                V((2, NP - NF, WX + 2, WY + 16, D), f32),
+                V((NF, WX + 2, WY + 16, D), f32),
+                V((NF, WX + 2, WY + 16, D), f32),
+                V((NP - NF, WX + 2, WY + 16, D), f32),
+                V((NP - NF, WX + 2, WY + 16, D), f32),
                 V((3, WX + 2, WY + 16, D), f32),
                 V((2, WY + 16, D), f32),
                 V((2, WX, WY + 8, D), f32),

time: 58.4 us -> 48.8 us (0.84)
  Pallas kernels: 53.2 us -> 43.7 us
    pallas_call x1, Pallas kernels: 53.2 us -> 43.7 us  [per_device(): pl.pallas_call(functools.partial(kernel, sizes, steps), out_shape=(jax.Sh...]
where the time goes in v4:
time: 48.8 us; the launch traced here: 48.7 us
  Pallas kernels  43.7 us (90%)
  local copies, waits for them, and re-layouts  4.38 us (9%)
  between operations  0.65 us (1%)
    pallas_call x1, Pallas kernels, per_device(): pl.pallas_call(functools.partial(kernel, sizes, steps), out_shape=(jax.Sh...  43.7 us
    unnamed x4, local copies, waits for them, and re-layouts  4.38 us

profile of v4, /device:TPU:88, one launch (start us, length us, event | category | flops | bytes accessed | tf_op | source)
XLA Modules:
  0.0 48.7 jit_solution(3818308472180938187)
XLA Ops:
  0.6 43.7 %shard_map.86 = (f32[19,16,16,128]{3,2,1,0:T(8,128)}, f32[7,16,16,128]{3,2,1,0:T(8,128)}) custom-call(s32[64]{0:T(128)} %owner_ref.1, f32[19,16,16,128]{3,2,1,0:T(8,128)} %flow_hbm.1, f32[7,16,16,128]{3,2,1,0:T(8,128)} %sol_hbm.1, bf16[4,16,16,128]{3,2,1,0:T(8,128)(2,1)} %rho_hbm.1, bf16[4,3,16,16,128]{4,3,2,1,0:T(8,128)(2,1)} %vel_hbm.1, ...), custom_call_target="tpu_custom_call" | custom-call | tf_op jit(solution)/shard_map/pallas_call | solution.py:613
  44.3 0.0 copy-start
  44.3 3.4 %copy.11 = f32[19,16,16,128]{3,2,1,0:T(8,128)} copy(f32[19,16,16,128]{3,2,1,0:T(8,128)} %get-tuple-element.4) | data formatting | bytes 4980736
  47.8 0.0 copy-done
  47.8 0.9 %copy.12 = f32[7,16,16,128]{3,2,1,0:T(8,128)} copy(f32[7,16,16,128]{3,2,1,0:T(8,128)S(1)} %copy-done) | data formatting | bytes 1835008
Async XLA Ops:
  44.3 3.5 %copy-start = (f32[7,16,16,128]{3,2,1,0:T(8,128)S(1)}, f32[7,16,16,128]{3,2,1,0:T(8,128)}, u32[]{:S(2)}) copy-start(f32[7,16,16,128]{3,2,1,0:T(8,128)} %get-tuple-element.5) | copy-start | bytes 2752516

commit v5 on v4

--- a/solution.py
+++ b/solution.py
@@ -166,7 +166,7 @@
     row = lax.broadcasted_iota(jnp.int32, (8, D), 0)
     edge = (lane == top, lane == 0)
     last_column = SPAN - 2
-    slot_lane = (lane - last_column, (lane - (top + last_column) + 2 * D) % D)
+    slot_lane = (lane - last_column, lax.rem(lane - (top + last_column - SPAN) + 2 * D, D) - SPAN)
 
     n = [
         (me[a] > 0).astype(jnp.int32) + (me[a] < sizes[a] - 1).astype(jnp.int32) for a in range(3)
@@ -259,7 +259,7 @@
     def over_x(body, init, unroll):
         def trip(i, carry):
             for j in range(unroll):
-                carry = body(unroll * i + j, carry)
+                carry = body(unroll * i + j, carry, j, unroll)
             return carry
 
         return lax.fori_loop(0, WX // unroll, trip, init)
@@ -267,11 +267,13 @@
     def edge_row(value, s):
         return value[0:1] if s == 0 else value[7:8]
 
-    def pack(acc, s, values):
-        acc = pltpu.roll(acc, D - 1, 1)
+    def pack(acc, s, values, j, unroll):
+        if j == 0:
+            acc = pltpu.roll(acc, D - unroll, 1)
+        back = unroll - 1 - j
         for q, value in enumerate(values):
-            moved = pltpu.roll(value, q * SPAN + last_column, 1)
-            acc = jnp.where(slot_lane[s] == q * SPAN, moved, acc)
+            moved = pltpu.roll(value, q * SPAN + last_column - back, 1)
+            acc = jnp.where(slot_lane[s] == q * SPAN - back, moved, acc)
         return acc
 
     def settle(face, s):
@@ -374,21 +376,21 @@
 
     blank = (zero,) * (2 * H)
 
-    def stage_tile(slot, x, h, values, packed, flag=None):
+    def stage_tile(slot, x, h, values, packed, trip, flag=None):
         extra = [] if flag is None else [flag]
         for s in (0, 1):
             if h == (0 if s == 0 else H - 1):
                 for q, value in enumerate([values[p] for p in FACE[1][s]] + extra):
                     sy[slot, s, q, pl.ds(x, 1), :] = edge_row(value, s)
             i = s * H + h
-            packed[i] = pack(packed[i], s, [values[p] for p in FACE[2][s]] + extra)
-
-    def stage_sol_tile(slot, x, h, values, packed):
+            packed[i] = pack(packed[i], s, [values[p] for p in FACE[2][s]] + extra, *trip)
+
+    def stage_sol_tile(slot, x, h, values, packed, trip):
         for s in (0, 1):
             if h == (0 if s == 0 else H - 1):
                 ty[slot, s, pl.ds(x, 1), :] = edge_row(values[3 + s], s)
             i = s * H + h
-            packed[i] = pack(packed[i], s, [values[5 + s]])
+            packed[i] = pack(packed[i], s, [values[5 + s]], *trip)
 
     def stage_sol(slot, cur, packed):
         for s in (0, 1):
@@ -403,17 +405,17 @@
         def __getitem__(self, p):
             return self.ref[p, self.x + 1, self.part, :]
 
-    def first_stage(x, packed):
+    def first_stage(x, packed, *trip):
         packed, other = list(packed[0]), list(packed[1])
         flags = solid[x].astype(jnp.float32)
         S[0, x + 1, pl.ds(Y0, WY), :] = flags
         for h in range(H):
             part = pl.ds(Y0 + 8 * h, 8)
-            stage_tile(0, x, h, Tiles(A0, x, part), packed, flags[8 * h : 8 * h + 8])
-            stage_sol_tile(0, x, h, Tiles(B0, x, part), other)
+            stage_tile(0, x, h, Tiles(A0, x, part), packed, trip, flags[8 * h : 8 * h + 8])
+            stage_sol_tile(0, x, h, Tiles(B0, x, part), other, trip)
         return tuple(packed), tuple(other)
 
-    packed, other = over_x(first_stage, (blank, blank), 2)
+    packed, other = over_x(first_stage, (blank, blank), 4)
     stage_flow(0, True, 0, packed)
     send_flow(0, True)
     stage_sol(0, 0, other)
@@ -449,7 +451,7 @@
                 face = uz[slot, s, pl.ds(8 * h, 8), :]
                 halo.append(pltpu.roll(face, top - 1 if s == 0 else D - 1, 1))
 
-        def body(x, carry):
+        def body(x, carry, *trip):
             halo, packed = list(carry[0]), list(carry[1])
             level_ = lev[t, x].astype(jnp.float32)
             density_ = rho[t, x].astype(jnp.float32)
@@ -482,7 +484,7 @@
                 new = [(1.0 - solute_omega) * v + common for v in hs]
                 for p in range(7):
                     B[nxt][p, x + 1, here, :] = new[p]
-                stage_sol_tile(nxt, x, h, new, packed)
+                stage_sol_tile(nxt, x, h, new, packed, trip)
                 factor = (0.5 * solute_omega) * level * (1.0 / density)
                 speed = u[0] * u[0] + u[1] * u[1] + u[2] * u[2]
                 saved = [factor * mx, factor * my, factor * mz, factor * along]
@@ -493,7 +495,7 @@
         _, packed = over_x(body, (tuple(halo), blank), U_SOL)
         stage_sol(nxt, nxt, packed)
 
-    def flow_tile(cur, x, h):
+    def flow_tile(cur, x, h, sign=1.0):
         start = Y0 + 8 * h
 
         def read(p):
@@ -532,12 +534,14 @@
         vy = qxy * ux + qyy * uy + qyz * uz
         vz = qxz * ux + qyz * uy + qzz * uz
         quad = vx * ux + vy * uy + vz * uz
-        w = flow_omega / 36.0
+        w = sign * flow_omega / 36.0
+        if sign < 0:
+            px, py, pz, along = -px, -py, -pz, -along
         scalar = w * (total * stretch - 4.5 * quad) - along
         tx_ = (3.0 * w) * (jx + 3.0 * vx - ux * total) + px
         ty_ = (3.0 * w) * (jy + 3.0 * vy - uy * total) + py
         tz_ = (3.0 * w) * (jz + 3.0 * vz - uz * total) + pz
-        rest = 1.0 - flow_omega
+        rest = sign * (1.0 - flow_omega)
         new = [rest * g[0] + scalar]
         pairs = [tx_, ty_, tz_, tx_ + ty_, tx_ - ty_, tx_ + tz_, tx_ - tz_, ty_ + tz_, ty_ - tz_]
         for i, v in enumerate(pairs):
@@ -553,13 +557,13 @@
         cur = k % 2
         nxt = 1 - cur
 
-        def body(x, packed):
+        def body(x, packed, *trip):
             packed = list(packed)
             for h in range(H):
                 new = flow_tile(cur, x, h)
                 for p in range(NF):
                     A[nxt][p, x + 1, pl.ds(Y0 + 8 * h, 8), :] = new[p]
-                stage_tile(nxt, x, h, new, packed)
+                stage_tile(nxt, x, h, new, packed, trip)
             return tuple(packed)
 
         packed = over_x(body, blank, U_FLOW)
@@ -574,16 +578,16 @@
     for k in range(steps - 1):
         step(k)
 
-    def last(x, carry):
+    def last(x, carry, *trip):
         for h in range(H):
-            new = flow_tile((steps - 1) % 2, x, h)
+            new = flow_tile((steps - 1) % 2, x, h, -1.0)
             part = pl.ds(8 * h, 8)
             here = pl.ds(Y0 + 8 * h, 8)
             keep = (S[0, x + 1, here, :] < 0.5) & (lane <= top)
             for p in range(NF):
                 oflow[p, x, part, :] = jnp.where(keep, new[p], 0.0)
             for p in range(NP - NF):
-                osol[p, x, part, :] = jnp.where(keep, B[steps % 2][p, x + 1, here, :], 0.0)
+                osol[p, x, part, :] = jnp.where(keep, -B[steps % 2][p, x + 1, here, :], 0.0)
         return carry
 
     over_x(last, 0, U_FLOW)
@@ -599,7 +603,7 @@
         f32 = jnp.float32
         V = pltpu.VMEM
         DMA = pltpu.SemaphoreType.DMA
-        hbm = pl.BlockSpec(memory_space=pl.ANY)
+        hbm = pl.BlockSpec(memory_space=pltpu.HBM)
         n = len(NBR) + len(FACES)
         faces = [
             V((2, 2, NQ + 1, WY, D), f32),
@@ -610,11 +614,11 @@
             V((2, 4, 1, D), f32),
         ]
         sides = [V((2, 2, WY, D), f32), V((2, 2, WX, D), f32), V((2, 2, WY, D), f32)]
-        return pl.pallas_call(
+        minus_flow, minus_sol = pl.pallas_call(
             functools.partial(kernel, sizes, steps),
             out_shape=(
-                jax.ShapeDtypeStruct(flow.shape, f32),
-                jax.ShapeDtypeStruct(solute.shape, f32),
+                pltpu.VMEM(flow.shape, f32),
+                pltpu.VMEM(solute.shape, f32),
             ),
             in_specs=[pl.BlockSpec(memory_space=pltpu.SMEM)] + [hbm] * 6,
             out_specs=(pl.BlockSpec(memory_space=pltpu.VMEM),) * 2,
@@ -638,6 +642,7 @@
                 collective_id=0, has_side_effects=True, vmem_limit_bytes=60 * 2**20
             ),
         )(owner, flow, solute, rho, vel, lev, solid)
+        return -minus_flow, -minus_sol
 
     field = P(None, "gx", "gy", "gz")
     return jax.shard_map(

time: 48.8 us -> 44.7 us (0.916)
  local copies, waits for them, and re-layouts: 4.38 us -> 0 us
  other arithmetic: 0 us -> 2.7 us
  Pallas kernels: 43.7 us -> 41.3 us
    unnamed x4 -> x0, local copies, waits for them, and re-layouts: 4.38 us -> none
    neg x0 -> x2, other arithmetic: none -> 2.7 us  [per_device(): return (-minus_flow, -minus_sol)]
    pallas_call x1, Pallas kernels: 43.7 us -> 41.3 us  [per_device(): pl.pallas_call(functools.partial(kernel, sizes, steps), out_shape=(pltpu....]
where the time goes in v5:
time: 44.7 us; the launch traced here: 44.6 us
  Pallas kernels  41.3 us (92%)
  other arithmetic  2.7 us (6%)
  between operations  0.64 us (1%)
    pallas_call x1, Pallas kernels, per_device(): pl.pallas_call(functools.partial(kernel, sizes, steps), out_shape=(pltpu....  41.3 us
    neg x2, other arithmetic, per_device(): return (-minus_flow, -minus_sol)  2.7 us

profile of v5, /device:TPU:88, one launch (start us, length us, event | category | flops | bytes accessed | tf_op | source)
XLA Modules:
  0.0 44.6 jit_solution(4432295032188407560)
XLA Ops:
  0.6 41.3 %shard_map.86 = (f32[19,16,16,128]{3,2,1,0:T(8,128)S(1)}, f32[7,16,16,128]{3,2,1,0:T(8,128)S(1)}) custom-call(s32[64]{0:T(128)} %owner_ref.1, f32[19,16,16,128]{3,2,1,0:T(8,128)} %flow_hbm.1, f32[7,16,16,128]{3,2,1,0:T(8,128)} %sol_hbm.1, bf16[4,16,16,128]{3,2,1,0:T(8,128)(2,1)} %rho_hbm.1, bf16[4,3,16,16,128]{4,3,2,1,0:T(8,128)(2,1)} %vel_hbm.1, ...), custom_call_target="tpu_custom_call" | custom-call | tf_op jit(solution)/shard_map/pallas_call | solution.py:617
  41.9 1.7 %neg.6 = f32[19,16,16,128]{3,2,1,0:T(8,128)} negate(f32[19,16,16,128]{3,2,1,0:T(8,128)S(1)} %get-tuple-element.4) | non-fusion elementwise | flops 622592 | bytes 4980736 | tf_op jit(solution)/shard_map/neg | solution.py:645
  43.6 1.0 %neg.7 = f32[7,16,16,128]{3,2,1,0:T(8,128)} negate(f32[7,16,16,128]{3,2,1,0:T(8,128)S(1)} %get-tuple-element.5) | non-fusion elementwise | flops 229376 | bytes 1835008 | tf_op jit(solution)/shard_map/neg | solution.py:645

commit v6 on v5

--- a/solution.py
+++ b/solution.py
@@ -51,8 +51,10 @@
 XZ = [c for c in NBR if c[0] and c[2]]
 YZ = [c for c in NBR if c[1] and c[2]]
 FLAT = [c for c in NBR if not c[2]]
+INNER = [c for c in NBR if not c[0]]
 UPDOWN = [c for c in NBR if c[2]]
-U_FLOW, U_SOL = 2, 4
+U_SOL = 4
+OUTER = (5, 4, 3, 2)
 Y0 = 8
 
 
@@ -166,7 +168,7 @@
     row = lax.broadcasted_iota(jnp.int32, (8, D), 0)
     edge = (lane == top, lane == 0)
     last_column = SPAN - 2
-    slot_lane = (lane - last_column, lax.rem(lane - (top + last_column - SPAN) + 2 * D, D) - SPAN)
+    slot_lane = (lane, lax.rem(lane - top + 2 * D, D))
 
     n = [
         (me[a] > 0).astype(jnp.int32) + (me[a] < sizes[a] - 1).astype(jnp.int32) for a in range(3)
@@ -175,7 +177,7 @@
         barrier, n[0] + n[1] + n[2] + n[0] * n[1] + n[0] * n[2] + n[1] * n[2]
     )
 
-    def flow_refs(c, slot, first):
+    def flow_refs(c, slot, first, phase=0, span=None):
         nq = NQ + 1 if first else NQ
         if c in XY:
             part = (slot, XY.index(c), pl.ds(0, nq - NQ + 1))
@@ -184,18 +186,21 @@
             part = (slot, XZ.index(c))
             return sxz.at[part], rxz.at[part]
         if c in YZ:
-            part = (slot, YZ.index(c))
+            part = (slot, phase, YZ.index(c))
             return syz.at[part], ryz.at[part]
         a = axis(c)
-        part = (slot, side(c[a]))
         if a == 2:
+            part = (slot, phase, side(c[a]))
             return sz.at[part], rz.at[part]
-        part = part + (pl.ds(0, nq),)
-        return ((sx, rx), (sy, ry))[a][0].at[part], ((sx, rx), (sy, ry))[a][1].at[part]
-
-    def flow_message(c, slot, first):
-        src, dst = flow_refs(c, slot, first)
-        i = NBR.index(c)
+        part = (slot, side(c[a]), pl.ds(0, nq))
+        if a == 0:
+            return sx.at[part], rx.at[part]
+        part = part + (pl.ds(2 * span[0], 2 * (span[1] - span[0])),)
+        return sy.at[part], ry.at[part]
+
+    def flow_message(c, slot, first, phase, span):
+        src, dst = flow_refs(c, slot, first, phase, span)
+        i = INNER.index(c) + len(NBR) if phase else NBR.index(c)
         return pltpu.make_async_remote_copy(
             src_ref=src,
             dst_ref=dst,
@@ -208,7 +213,7 @@
     def sol_message(c, slot):
         a = axis(c)
         part = (slot, side(c[a]))
-        i = len(NBR) + FACES.index(c)
+        i = len(NBR) + len(INNER) + FACES.index(c)
         return pltpu.make_async_remote_copy(
             src_ref=(tx, ty, tz)[a].at[part],
             dst_ref=(ux, uy, uz)[a].at[part],
@@ -227,15 +232,19 @@
 
     same = lambda c: c
 
-    def send_flow(slot, first):
-        each(NBR, neg, lambda c: flow_message(c, slot, first).start())
-
-    def wait_flow(slot, first):
-        each(NBR, neg, lambda c: flow_message(c, slot, first).wait_send())
-        each(FLAT, same, lambda c: flow_message(c, slot, first).wait_recv())
-        merge_flat(slot, first, slot)
-        each(UPDOWN, same, lambda c: flow_message(c, slot, first).wait_recv())
-        merge_z(slot, first)
+    def send_flow(slot, first, phase, span):
+        table = INNER if phase else NBR
+        each(table, neg, lambda c: flow_message(c, slot, first, phase, span).start())
+
+    def wait_flow(slot, first, phase, span, xs):
+        table = INNER if phase else NBR
+        each(table, neg, lambda c: flow_message(c, slot, first, phase, span).wait_send())
+        flat = [c for c in table if not c[2]]
+        each(flat, same, lambda c: flow_message(c, slot, first, phase, span).wait_recv())
+        merge_flat(slot, first, slot, phase, span)
+        far = [c for c in table if c[2]]
+        each(far, same, lambda c: flow_message(c, slot, first, phase, span).wait_recv())
+        merge_z(slot, first, phase, xs)
 
     def send_sol(slot):
         each(FACES, neg, lambda c: sol_message(c, slot).start())
@@ -250,7 +259,7 @@
             @pl.when(jnp.logical_not(exists(c)))
             def _(c=c):
                 for k in range(2):
-                    refs = [flow_refs(c, k, True)[1]]
+                    refs = [flow_refs(c, k, True, f, (0, WX // 2))[1] for f in (0, 1)]
                     if c in FACES:
                         refs.append((ux, uy, uz)[axis(c)].at[k, side(c[axis(c)])])
                     for ref in refs:
@@ -270,23 +279,28 @@
     def pack(acc, s, values, j, unroll):
         if j == 0:
             acc = pltpu.roll(acc, D - unroll, 1)
-        back = unroll - 1 - j
+        return put_lanes(acc, s, values, last_column - (unroll - 1 - j))
+
+    def put_lanes(acc, s, values, at):
         for q, value in enumerate(values):
-            moved = pltpu.roll(value, q * SPAN + last_column - back, 1)
-            acc = jnp.where(slot_lane[s] == q * SPAN - back, moved, acc)
+            moved = pltpu.roll(value, q * SPAN + at, 1)
+            acc = jnp.where(slot_lane[s] == q * SPAN + at, moved, acc)
         return acc
 
     def settle(face, s):
         return face if s == 0 else pltpu.roll(face, D - top, 1)
 
-    def stage_flow(slot, first, cur, packed):
-        for s in (0, 1):
-            face = [settle(packed[s * H + h], s) for h in range(H)]
+    def stage_flow(slot, first, cur, packed, phase):
+        for s in (0, 1):
+            low, high = packed[: 2 * H], packed[2 * H :]
+            face = [settle(low[s * H + h] + high[s * H + h], s) for h in range(H)]
             for h in range(H):
-                sz[slot, s, pl.ds(8 * h, 8), :] = face[h]
+                sz[slot, phase, s, pl.ds(8 * h, 8), :] = face[h]
             for d, c in enumerate(YZ):
                 if side(c[2]) == s:
-                    syz[slot, d] = face[0][0:1] if c[1] > 0 else face[H - 1][7:8]
+                    syz[slot, phase, d] = face[0][0:1] if c[1] > 0 else face[H - 1][7:8]
+            if phase:
+                continue
             for d, c in enumerate(XZ):
                 if side(c[2]) == s:
                     column = 1 if c[0] > 0 else WX
@@ -298,6 +312,8 @@
                             value = jnp.broadcast_to(face[h][:, i : i + 1], (8, D))
                             line = jnp.where(lane == row + (WY * at + 8 * h), value, line)
                     sxz[slot, d] = jnp.sum(line, axis=0, keepdims=True)
+        if phase:
+            return
         for s in (0, 1):
             x = 1 if s == 0 else WX
             for q, p in enumerate(FACE[0][s]):
@@ -306,16 +322,16 @@
                 sx[slot, s, NQ] = S[0, x, pl.ds(Y0, WY), :]
         for d, c in enumerate(XY):
             q = FACE[1][side(c[1])].index(FLOW_DIRS.index(c))
-            x = 0 if c[0] > 0 else WX - 1
-            sxy[slot, d, 0] = sy[slot, side(c[1]), q, pl.ds(x, 1), :]
+            r = 0 if c[0] > 0 else 1
+            sxy[slot, d, 0] = sy[slot, side(c[1]), q, r]
             if first:
-                sxy[slot, d, 1] = sy[slot, side(c[1]), NQ, pl.ds(x, 1), :]
+                sxy[slot, d, 1] = sy[slot, side(c[1]), NQ, r]
 
     def column_of(line, start):
         line = jnp.broadcast_to(line, (8, D))
         return jnp.sum(jnp.where(lane == row + start, line, 0.0), axis=1, keepdims=True)
 
-    def merge_flat(slot, first, cur):
+    def merge_flat(slot, first, cur, phase, span):
         flag = [(NQ, None)] if first else []
 
         def put(p, x, rows, value):
@@ -325,15 +341,17 @@
                 A[cur][p, x, rows, :] = value
 
         for s in (0, 1):
-            x = WX + 1 if s == 0 else 0
-            for q, p in list(enumerate(FACE[0][s])) + flag:
-                put(p, x, pl.ds(Y0, WY), rx[slot, s, q])
+            if not phase:
+                x = WX + 1 if s == 0 else 0
+                for q, p in list(enumerate(FACE[0][s])) + flag:
+                    put(p, x, pl.ds(Y0, WY), rx[slot, s, q])
             y = Y0 + WY if s == 0 else Y0 - 1
             for q, p in list(enumerate(FACE[1][s])) + flag:
-                for half in range(WX // 8):
-                    value = ry[slot, s, q, pl.ds(8 * half, 8), :]
-                    for i in range(8):
-                        put(p, 1 + 8 * half + i, pl.ds(y, 1), value[i : i + 1])
+                for r in range(2 * span[0], 2 * span[1]):
+                    x = WX - 1 - r // 2 if r % 2 else r // 2
+                    put(p, 1 + x, pl.ds(y, 1), ry[slot, s, q, r])
+        if phase:
+            return
         for d, c in enumerate(XY):
             x = WX + 1 if c[0] > 0 else 0
             y = Y0 + WY if c[1] > 0 else Y0 - 1
@@ -341,26 +359,31 @@
             if first:
                 put(None, x, pl.ds(y, 1), rxy[slot, d, 1])
 
-    def merge_z(slot, first):
+    def merge_z(slot, first, phase, xs):
         for s in (0, 1):
             cz = 1 - 2 * s
             turn = (lambda v: pltpu.roll(v, top, 1)) if s == 0 else (lambda v: v)
             for h in range(H):
-                face = rz[slot, s, pl.ds(8 * h, 8), :]
-                for cx in (1, -1):
-                    c = (cx, 0, cz)
-                    q = FACE[2][s].index(FLOW_DIRS.index(c))
-                    for at, qz in enumerate((q, NQ) if first else (q,)):
-                        value = column_of(rxz[slot, XZ.index(c)], WY * at + 8 * h)
-                        i = qz * SPAN + (WX + 1 if cx > 0 else 0)
-                        face = jnp.where(lane == i, value, face)
-                Zf[s, pl.ds(Y0 + 8 * h, 8), :] = turn(face)
+                part = pl.ds(Y0 + 8 * h, 8)
+                face = rz[slot, phase, s, pl.ds(8 * h, 8), :]
+                if not phase:
+                    for cx in (1, -1):
+                        c = (cx, 0, cz)
+                        q = FACE[2][s].index(FLOW_DIRS.index(c))
+                        for at, qz in enumerate((q, NQ) if first else (q,)):
+                            value = column_of(rxz[slot, XZ.index(c)], WY * at + 8 * h)
+                            i = qz * SPAN + (WX + 1 if cx > 0 else 0)
+                            face = jnp.where(lane == i, value, face)
+                    Zf[s, part, :] = turn(face)
+                else:
+                    Zf[s, part, :] = Zf[s, part, :] + turn(face)
             for y, cy in ((Y0 + WY, 1), (Y0 - 1, -1)):
-                line = jnp.broadcast_to(ryz[slot, YZ.index((0, cy, cz))], (8, D))
-                Zf[s, pl.ds(y, 1), :] = turn(line)[0:1]
+                line = jnp.broadcast_to(ryz[slot, phase, YZ.index((0, cy, cz))], (8, D))
+                line = turn(line)[0:1]
+                Zf[s, pl.ds(y, 1), :] = Zf[s, pl.ds(y, 1), :] + line if phase else line
             for t in range(3):
                 face = Zf[s, pl.ds(Y0 - 1 + 8 * t, 8), :]
-                for x in range(WX):
+                for x in xs:
                     ZR[s, x, pl.ds(8 * t, 8), :] = pltpu.roll(face, D - x, 1) if x else face
 
     for c in copies[:6]:
@@ -376,14 +399,16 @@
 
     blank = (zero,) * (2 * H)
 
-    def stage_tile(slot, x, h, values, packed, trip, flag=None):
+    def stage_tile(slot, i, b, h, values, packed, end, flag=None):
         extra = [] if flag is None else [flag]
         for s in (0, 1):
             if h == (0 if s == 0 else H - 1):
                 for q, value in enumerate([values[p] for p in FACE[1][s]] + extra):
-                    sy[slot, s, q, pl.ds(x, 1), :] = edge_row(value, s)
-            i = s * H + h
-            packed[i] = pack(packed[i], s, [values[p] for p in FACE[2][s]] + extra, *trip)
+                    sy[slot, s, q, 2 * i + b] = edge_row(value, s)
+            at = b * 2 * H + s * H + h
+            acc = pltpu.roll(packed[at], 1 if b else D - 1, 1)
+            values_z = [values[p] for p in FACE[2][s]] + extra
+            packed[at] = put_lanes(acc, s, values_z, WX + 1 - end if b else end)
 
     def stage_sol_tile(slot, x, h, values, packed, trip):
         for s in (0, 1):
@@ -405,25 +430,35 @@
         def __getitem__(self, p):
             return self.ref[p, self.x + 1, self.part, :]
 
-    def first_stage(x, packed, *trip):
-        packed, other = list(packed[0]), list(packed[1])
-        flags = solid[x].astype(jnp.float32)
-        S[0, x + 1, pl.ds(Y0, WY), :] = flags
+    def first_stage(i, packed):
+        packed = list(packed)
+        for b in (0, 1):
+            x = WX - 1 - i if b else i
+            flags = solid[x].astype(jnp.float32)
+            S[0, x + 1, pl.ds(Y0, WY), :] = flags
+            for h in range(H):
+                part = pl.ds(Y0 + 8 * h, 8)
+                flag = flags[8 * h : 8 * h + 8]
+                stage_tile(0, i, b, h, Tiles(A0, x, part), packed, WX // 2, flag)
+        return tuple(packed)
+
+    def first_sol(x, other, *trip):
+        other = list(other)
         for h in range(H):
-            part = pl.ds(Y0 + 8 * h, 8)
-            stage_tile(0, x, h, Tiles(A0, x, part), packed, trip, flags[8 * h : 8 * h + 8])
-            stage_sol_tile(0, x, h, Tiles(B0, x, part), other, trip)
-        return tuple(packed), tuple(other)
-
-    packed, other = over_x(first_stage, (blank, blank), 4)
-    stage_flow(0, True, 0, packed)
-    send_flow(0, True)
+            stage_sol_tile(0, x, h, Tiles(B0, x, pl.ds(Y0 + 8 * h, 8)), other, trip)
+        return tuple(other)
+
+    whole = (0, WX // 2)
+    packed = lax.fori_loop(0, WX // 2, first_stage, blank * 2)
+    stage_flow(0, True, 0, packed, 0)
+    send_flow(0, True, 0, whole)
+    other = over_x(first_sol, blank, 4)
     stage_sol(0, 0, other)
     send_sol(0)
     clear_missing()
     for c in copies[6:]:
         c.wait()
-    wait_flow(0, True)
+    wait_flow(0, True, 0, whole, range(WX))
     for x in range(WX + 2):
         for t in range(0, WY + 16, 8):
             part = pl.ds(t, 8)
@@ -553,44 +588,58 @@
     solute_step(0, 0)
     send_sol(1)
 
-    def step(k):
+    def outer_slabs(k):
+        return [x for x in range(WX) if x < OUTER[k] or x >= WX - OUTER[k]]
+
+    def flow_phase(k, phase):
         cur = k % 2
         nxt = 1 - cur
-
-        def body(x, packed, *trip):
+        span = (OUTER[k], WX // 2) if phase else (0, OUTER[k])
+
+        def body(i, packed):
             packed = list(packed)
-            for h in range(H):
-                new = flow_tile(cur, x, h)
-                for p in range(NF):
-                    A[nxt][p, x + 1, pl.ds(Y0 + 8 * h, 8), :] = new[p]
-                stage_tile(nxt, x, h, new, packed, trip)
+            for b in (0, 1):
+                x = WX - 1 - i if b else i
+                for h in range(H):
+                    if k < steps - 1:
+                        new = flow_tile(cur, x, h)
+                        for p in range(NF):
+                            A[nxt][p, x + 1, pl.ds(Y0 + 8 * h, 8), :] = new[p]
+                        stage_tile(nxt, i, b, h, new, packed, span[1])
+                    else:
+                        new = flow_tile(cur, x, h, -1.0)
+                        part = pl.ds(8 * h, 8)
+                        here = pl.ds(Y0 + 8 * h, 8)
+                        keep = (S[0, x + 1, here, :] < 0.5) & (lane <= top)
+                        for p in range(NF):
+                            oflow[p, x, part, :] = jnp.where(keep, new[p], 0.0)
+                        for p in range(NP - NF):
+                            osol[p, x, part, :] = jnp.where(
+                                keep, -B[steps % 2][p, x + 1, here, :], 0.0
+                            )
             return tuple(packed)
 
-        packed = over_x(body, blank, U_FLOW)
-        stage_flow(nxt, False, nxt, packed)
-        send_flow(nxt, False)
-        solute_step(k + 1, nxt)
-
-        if k < steps - 2:
-            send_sol(cur)
-        wait_flow(nxt, False)
-
-    for k in range(steps - 1):
-        step(k)
-
-    def last(x, carry, *trip):
-        for h in range(H):
-            new = flow_tile((steps - 1) % 2, x, h, -1.0)
-            part = pl.ds(8 * h, 8)
-            here = pl.ds(Y0 + 8 * h, 8)
-            keep = (S[0, x + 1, here, :] < 0.5) & (lane <= top)
-            for p in range(NF):
-                oflow[p, x, part, :] = jnp.where(keep, new[p], 0.0)
-            for p in range(NP - NF):
-                osol[p, x, part, :] = jnp.where(keep, -B[steps % 2][p, x + 1, here, :], 0.0)
-        return carry
-
-    over_x(last, 0, U_FLOW)
+        if k == steps - 1:
+            lax.fori_loop(span[0], span[1], lambda i, c: (body(i, ()), c)[1], 0)
+            return
+        packed = lax.fori_loop(span[0], span[1], body, blank * 2)
+        stage_flow(nxt, False, nxt, packed, phase)
+        send_flow(nxt, False, phase, span)
+
+    for k in range(steps):
+        slot = k % 2
+        outer = outer_slabs(k)
+        if k:
+            wait_flow(slot, False, 0, (0, OUTER[k - 1]), outer)
+        flow_phase(k, 0)
+        if k:
+            inner = [x for x in range(WX) if x not in outer]
+            wait_flow(slot, False, 1, (OUTER[k - 1], WX // 2), inner)
+        flow_phase(k, 1)
+        if k < steps - 1:
+            solute_step(k + 1, 1 - slot)
+            if k < steps - 2:
+                send_sol(slot)
 
 
 def solution(mesh):
@@ -604,14 +653,14 @@
         V = pltpu.VMEM
         DMA = pltpu.SemaphoreType.DMA
         hbm = pl.BlockSpec(memory_space=pltpu.HBM)
-        n = len(NBR) + len(FACES)
+        n = len(NBR) + len(INNER) + len(FACES)
         faces = [
             V((2, 2, NQ + 1, WY, D), f32),
-            V((2, 2, NQ + 1, WX, D), f32),
-            V((2, 2, WY, D), f32),
+            V((2, 2, NQ + 1, WX, 1, D), f32),
+            V((2, 2, 2, WY, D), f32),
             V((2, 4, 2, 1, D), f32),
             V((2, 4, 1, D), f32),
-            V((2, 4, 1, D), f32),
+            V((2, 2, 4, 1, D), f32),
         ]
         sides = [V((2, 2, WY, D), f32), V((2, 2, WX, D), f32), V((2, 2, WY, D), f32)]
         minus_flow, minus_sol = pl.pallas_call(

time: 44.7 us -> 43 us (0.962)
  Pallas kernels: 41.3 us -> 39.3 us
    pallas_call x1, Pallas kernels: 41.3 us -> 39.3 us  [per_device(): pl.pallas_call(functools.partial(kernel, sizes, steps), out_shape=(pltpu....]
where the time goes in v6:
time: 43 us; the launch traced here: 42.6 us
  Pallas kernels  39.3 us (91%)
  other arithmetic  2.7 us (6%)
  between operations  0.64 us (1%)
    pallas_call x1, Pallas kernels, per_device(): pl.pallas_call(functools.partial(kernel, sizes, steps), out_shape=(pltpu....  39.3 us
    neg x2, other arithmetic, per_device(): return (-minus_flow, -minus_sol)  2.7 us

profile of v6, /device:TPU:88, one launch (start us, length us, event | category | flops | bytes accessed | tf_op | source)
XLA Modules:
  0.0 42.6 jit_solution(4499773625873833471)
XLA Ops:
  0.6 39.3 %shard_map.86 = (f32[19,16,16,128]{3,2,1,0:T(8,128)S(1)}, f32[7,16,16,128]{3,2,1,0:T(8,128)S(1)}) custom-call(s32[64]{0:T(128)} %owner_ref.1, f32[19,16,16,128]{3,2,1,0:T(8,128)} %flow_hbm.1, f32[7,16,16,128]{3,2,1,0:T(8,128)} %sol_hbm.1, bf16[4,16,16,128]{3,2,1,0:T(8,128)(2,1)} %rho_hbm.1, bf16[4,3,16,16,128]{4,3,2,1,0:T(8,128)(2,1)} %vel_hbm.1, ...), custom_call_target="tpu_custom_call" | custom-call | tf_op jit(solution)/shard_map/pallas_call | solution.py:666
  39.9 1.7 %neg.6 = f32[19,16,16,128]{3,2,1,0:T(8,128)} negate(f32[19,16,16,128]{3,2,1,0:T(8,128)S(1)} %get-tuple-element.4) | non-fusion elementwise | flops 622592 | bytes 4980736 | tf_op jit(solution)/shard_map/neg | solution.py:694
  41.6 1.0 %neg.7 = f32[7,16,16,128]{3,2,1,0:T(8,128)} negate(f32[7,16,16,128]{3,2,1,0:T(8,128)S(1)} %get-tuple-element.5) | non-fusion elementwise | flops 229376 | bytes 1835008 | tf_op jit(solution)/shard_map/neg | solution.py:694

commit v7 on v6

--- a/solution.py
+++ b/solution.py
@@ -170,13 +170,6 @@
     last_column = SPAN - 2
     slot_lane = (lane, lax.rem(lane - top + 2 * D, D))
 
-    n = [
-        (me[a] > 0).astype(jnp.int32) + (me[a] < sizes[a] - 1).astype(jnp.int32) for a in range(3)
-    ]
-    pl.semaphore_wait(
-        barrier, n[0] + n[1] + n[2] + n[0] * n[1] + n[0] * n[2] + n[1] * n[2]
-    )
-
     def flow_refs(c, slot, first, phase=0, span=None):
         nq = NQ + 1 if first else NQ
         if c in XY:
@@ -204,7 +197,7 @@
         return pltpu.make_async_remote_copy(
             src_ref=src,
             dst_ref=dst,
-            send_sem=send_sem.at[slot, i],
+            send_sem=send_sem.at[i],
             recv_sem=recv_sem.at[slot, i],
             device_id=device(neg(c)),
             device_id_type=MESH,
@@ -217,7 +210,7 @@
         return pltpu.make_async_remote_copy(
             src_ref=(tx, ty, tz)[a].at[part],
             dst_ref=(ux, uy, uz)[a].at[part],
-            send_sem=send_sem.at[slot, i],
+            send_sem=send_sem.at[i],
             recv_sem=recv_sem.at[slot, i],
             device_id=device(neg(c)),
             device_id_type=MESH,
@@ -451,6 +444,12 @@
     whole = (0, WX // 2)
     packed = lax.fori_loop(0, WX // 2, first_stage, blank * 2)
     stage_flow(0, True, 0, packed, 0)
+    n = [
+        (me[a] > 0).astype(jnp.int32) + (me[a] < sizes[a] - 1).astype(jnp.int32) for a in range(3)
+    ]
+    pl.semaphore_wait(
+        barrier, n[0] + n[1] + n[2] + n[0] * n[1] + n[0] * n[2] + n[1] * n[2]
+    )
     send_flow(0, True, 0, whole)
     other = over_x(first_sol, blank, 4)
     stage_sol(0, 0, other)
@@ -458,6 +457,11 @@
     clear_missing()
     for c in copies[6:]:
         c.wait()
+    own = [(x + 1, Y0 + 8 * h) for x in range(WX) for h in range(H)]
+    for x, t in own:
+        part = pl.ds(t, 8)
+        for s in (0, 1):
+            S[1 + s, x, part, :] = pltpu.roll(S[0, x, part, :], D - 1 if s == 0 else 1, 1)
     wait_flow(0, True, 0, whole, range(WX))
     for x in range(WX + 2):
         for t in range(0, WY + 16, 8):
@@ -465,7 +469,10 @@
             flag = S[0, x, part, :]
             for s in (0, 1):
                 halo = pltpu.roll(Zf[s, part, :], D - (NQ * SPAN + x), 1)
-                moved = pltpu.roll(flag, D - 1 if s == 0 else 1, 1)
+                if (x, t) in own:
+                    moved = S[1 + s, x, part, :]
+                else:
+                    moved = pltpu.roll(flag, D - 1 if s == 0 else 1, 1)
                 S[1 + s, x, part, :] = jnp.where(edge[s], halo, moved)
 
     def solute_step(j, slot):
@@ -686,7 +693,7 @@
                 V(solid.shape, solid.dtype),
             ]
             + (faces + sides) * 2
-            + [DMA((9,)), DMA((2, n)), DMA((2, n))],
+            + [DMA((9,)), DMA((n,)), DMA((2, n))],
             compiler_params=pltpu.CompilerParams(
                 collective_id=0, has_side_effects=True, vmem_limit_bytes=60 * 2**20
             ),

time: 43 us -> 41.5 us (0.965)
  Pallas kernels: 39.3 us -> 37.7 us
    pallas_call x1, Pallas kernels: 39.3 us -> 37.7 us  [per_device(): pl.pallas_call(functools.partial(kernel, sizes, steps), out_shape=(pltpu....]
where the time goes in v7:
time: 41.5 us; the launch traced here: 41.1 us
  Pallas kernels  37.7 us (91%)
  other arithmetic  2.7 us (7%)
  between operations  0.64 us (2%)
    pallas_call x1, Pallas kernels, per_device(): pl.pallas_call(functools.partial(kernel, sizes, steps), out_shape=(pltpu....  37.7 us
    neg x2, other arithmetic, per_device(): return (-minus_flow, -minus_sol)  2.7 us

profile of v7, /device:TPU:88, one launch (start us, length us, event | category | flops | bytes accessed | tf_op | source)
XLA Modules:
  0.0 41.1 jit_solution(8187803585325441690)
XLA Ops:
  0.6 37.7 %shard_map.86 = (f32[19,16,16,128]{3,2,1,0:T(8,128)S(1)}, f32[7,16,16,128]{3,2,1,0:T(8,128)S(1)}) custom-call(s32[64]{0:T(128)} %owner_ref.1, f32[19,16,16,128]{3,2,1,0:T(8,128)} %flow_hbm.1, f32[7,16,16,128]{3,2,1,0:T(8,128)} %sol_hbm.1, bf16[4,16,16,128]{3,2,1,0:T(8,128)(2,1)} %rho_hbm.1, bf16[4,3,16,16,128]{4,3,2,1,0:T(8,128)(2,1)} %vel_hbm.1, ...), custom_call_target="tpu_custom_call" | custom-call | tf_op jit(solution)/shard_map/pallas_call | solution.py:673
  38.4 1.7 %neg.6 = f32[19,16,16,128]{3,2,1,0:T(8,128)} negate(f32[19,16,16,128]{3,2,1,0:T(8,128)S(1)} %get-tuple-element.4) | non-fusion elementwise | flops 622592 | bytes 4980736 | tf_op jit(solution)/shard_map/neg | solution.py:701
  40.0 1.0 %neg.7 = f32[7,16,16,128]{3,2,1,0:T(8,128)} negate(f32[7,16,16,128]{3,2,1,0:T(8,128)S(1)} %get-tuple-element.5) | non-fusion elementwise | flops 229376 | bytes 1835008 | tf_op jit(solution)/shard_map/neg | solution.py:701

commit v8 on v7

--- a/solution.py
+++ b/solution.py
@@ -457,23 +457,24 @@
     clear_missing()
     for c in copies[6:]:
         c.wait()
-    own = [(x + 1, Y0 + 8 * h) for x in range(WX) for h in range(H)]
-    for x, t in own:
-        part = pl.ds(t, 8)
-        for s in (0, 1):
-            S[1 + s, x, part, :] = pltpu.roll(S[0, x, part, :], D - 1 if s == 0 else 1, 1)
-    wait_flow(0, True, 0, whole, range(WX))
-    for x in range(WX + 2):
-        for t in range(0, WY + 16, 8):
-            part = pl.ds(t, 8)
-            flag = S[0, x, part, :]
-            for s in (0, 1):
-                halo = pltpu.roll(Zf[s, part, :], D - (NQ * SPAN + x), 1)
-                if (x, t) in own:
-                    moved = S[1 + s, x, part, :]
-                else:
-                    moved = pltpu.roll(flag, D - 1 if s == 0 else 1, 1)
-                S[1 + s, x, part, :] = jnp.where(edge[s], halo, moved)
+    def saved_tiles(t, x):
+        level_ = lev[t, x].astype(jnp.float32)
+        density_ = rho[t, x].astype(jnp.float32)
+        u_ = [vel[t, i, x].astype(jnp.float32) for i in range(3)]
+        for h in range(H):
+            cut = slice(8 * h, 8 * h + 8)
+            level, density, u = level_[cut], density_[cut], [v[cut] for v in u_]
+            one = 1.0 + level
+            sink = solute_omega - langmuir_rate / (one * one)
+            factor = (0.5 * solute_omega) * level * (1.0 / density)
+            speed = u[0] * u[0] + u[1] * u[1] + u[2] * u[2]
+            yield sink, factor, u, 1.0 + 1.5 * speed
+
+    def prepare(x, carry, *trip):
+        for h, (sink, factor, u, stretch) in enumerate(saved_tiles(steps - 1, x)):
+            for i, v in zip((0, 3, 4, 5, 6, 7), [sink, factor] + u + [stretch]):
+                PU[i, x, pl.ds(8 * h, 8), :] = v
+        return carry
 
     def solute_step(j, slot):
         t = steps - 1 - j
@@ -495,12 +496,15 @@
 
         def body(x, carry, *trip):
             halo, packed = list(carry[0]), list(carry[1])
-            level_ = lev[t, x].astype(jnp.float32)
-            density_ = rho[t, x].astype(jnp.float32)
-            u_ = [vel[t, i, x].astype(jnp.float32) for i in range(3)]
-            for h in range(H):
-                cut = slice(8 * h, 8 * h + 8)
-                level, density, u = level_[cut], density_[cut], [v[cut] for v in u_]
+            if j:
+                saved = list(saved_tiles(t, x))
+            else:
+                parts = [pl.ds(8 * h, 8) for h in range(H)]
+                saved = [
+                    (PU[0, x, r, :], PU[3, x, r, :], [PU[4 + i, x, r, :] for i in range(3)], None)
+                    for r in parts
+                ]
+            for h, (sink, factor, u, stretch) in enumerate(saved):
                 start = Y0 + 8 * h
                 here = pl.ds(start, 8)
                 hs = [B[cur][0, x + 1, here, :]]
@@ -519,23 +523,37 @@
                 mx, my, mz = hs[1] - hs[2], hs[3] - hs[4], hs[5] - hs[6]
                 m0 = 0.25 * hs[0] + 0.125 * ((hs[1] + hs[2]) + (hs[3] + hs[4]) + (hs[5] + hs[6]))
                 along = mx * u[0] + my * u[1] + mz * u[2]
-                one = 1.0 + level
-                common = (solute_omega - langmuir_rate / (one * one)) * m0 + (
-                    solute_omega * 0.5
-                ) * along
+                common = sink * m0 + (solute_omega * 0.5) * along
                 new = [(1.0 - solute_omega) * v + common for v in hs]
                 for p in range(7):
                     B[nxt][p, x + 1, here, :] = new[p]
                 stage_sol_tile(nxt, x, h, new, packed, trip)
-                factor = (0.5 * solute_omega) * level * (1.0 / density)
-                speed = u[0] * u[0] + u[1] * u[1] + u[2] * u[2]
-                saved = [factor * mx, factor * my, factor * mz, factor * along]
-                for i, v in enumerate(saved + u + [1.0 + 1.5 * speed]):
+                out = [factor * mx, factor * my, factor * mz, factor * along]
+                for i, v in enumerate(out + u + [stretch] if j else out):
                     PU[i, x, pl.ds(8 * h, 8), :] = v
             return tuple(pltpu.roll(v, D - 1, 1) for v in halo), tuple(packed)
 
         _, packed = over_x(body, (tuple(halo), blank), U_SOL)
         stage_sol(nxt, nxt, packed)
+
+    over_x(prepare, 0, 4)
+    own = [(x + 1, Y0 + 8 * h) for x in range(WX) for h in range(H)]
+    for x, t in own:
+        part = pl.ds(t, 8)
+        for s in (0, 1):
+            S[1 + s, x, part, :] = pltpu.roll(S[0, x, part, :], D - 1 if s == 0 else 1, 1)
+    wait_flow(0, True, 0, whole, range(WX))
+    for x in range(WX + 2):
+        for t in range(0, WY + 16, 8):
+            part = pl.ds(t, 8)
+            flag = S[0, x, part, :]
+            for s in (0, 1):
+                halo = pltpu.roll(Zf[s, part, :], D - (NQ * SPAN + x), 1)
+                if (x, t) in own:
+                    moved = S[1 + s, x, part, :]
+                else:
+                    moved = pltpu.roll(flag, D - 1 if s == 0 else 1, 1)
+                S[1 + s, x, part, :] = jnp.where(edge[s], halo, moved)
 
     def flow_tile(cur, x, h, sign=1.0):
         start = Y0 + 8 * h

time: 41.5 us -> 41.5 us (level)
  no operation moved by 1% of the time
where the time goes in v8:
time: 41.5 us; the launch traced here: 41 us
  Pallas kernels  37.7 us (91%)
  other arithmetic  2.7 us (7%)
  between operations  0.64 us (2%)
    pallas_call x1, Pallas kernels, per_device(): pl.pallas_call(functools.partial(kernel, sizes, steps), out_shape=(pltpu....  37.7 us
    neg x2, other arithmetic, per_device(): return (-minus_flow, -minus_sol)  2.7 us

profile of v8, /device:TPU:88, one launch (start us, length us, event | category | flops | bytes accessed | tf_op | source)
XLA Modules:
  0.0 41.0 jit_solution(5656678444043286792)
XLA Ops:
  0.6 37.7 %shard_map.86 = (f32[19,16,16,128]{3,2,1,0:T(8,128)S(1)}, f32[7,16,16,128]{3,2,1,0:T(8,128)S(1)}) custom-call(s32[64]{0:T(128)} %owner_ref.1, f32[19,16,16,128]{3,2,1,0:T(8,128)} %flow_hbm.1, f32[7,16,16,128]{3,2,1,0:T(8,128)} %sol_hbm.1, bf16[4,16,16,128]{3,2,1,0:T(8,128)(2,1)} %rho_hbm.1, bf16[4,3,16,16,128]{4,3,2,1,0:T(8,128)(2,1)} %vel_hbm.1, ...), custom_call_target="tpu_custom_call" | custom-call | tf_op jit(solution)/shard_map/pallas_call | solution.py:691
  38.4 1.7 %neg.6 = f32[19,16,16,128]{3,2,1,0:T(8,128)} negate(f32[19,16,16,128]{3,2,1,0:T(8,128)S(1)} %get-tuple-element.4) | non-fusion elementwise | flops 622592 | bytes 4980736 | tf_op jit(solution)/shard_map/neg | solution.py:719
  40.0 1.0 %neg.7 = f32[7,16,16,128]{3,2,1,0:T(8,128)} negate(f32[7,16,16,128]{3,2,1,0:T(8,128)S(1)} %get-tuple-element.5) | non-fusion elementwise | flops 229376 | bytes 1835008 | tf_op jit(solution)/shard_map/neg | solution.py:719
